TPU v7x, 512 devices: a whole 4x8x8 slice. The times are simulated.
512 devices in a mesh: grid: 128 (over y, z, core), tile: 4 (over x).
Axes of the slice: x: 4, y: 8, z: 8, core: 2. Of those that a mesh axis runs over, the one named last changes fastest.
Arguments:
- basis_values: bfloat16 [12288, 256, 128], P(('grid', 'tile')), may hold values from -6 to 6
- blocks: int32 [12288, 2], P(('grid', 'tile')), may hold values from 0 to 2, as said below
- counts: int32 [12288], P(('grid', 'tile')), may hold values from 1 to 256, as said below
- weighted_potential: float32 [12288, 256], P(('grid', 'tile')), may hold values from -0.12 to 0.12
- xc_kernel: float32 [12288, 256], P(('grid', 'tile')), may hold values from -0.002 to -0.0002
- occ_coef: bfloat16 [8192, 512], P('grid'), may hold values from -0.5 to 0.5
- virt_coef: bfloat16 [8192, 7680], P('grid', 'tile'), may hold values from -0.0625 to 0.0625
- occ_energy: float32 [512], replicated, may hold values from -2 to -0.5
- virt_energy: float32 [7680], P('tile'), may hold values from 0.3 to 8
Outputs:
- response_coef: bfloat16 [8192, 512], P('grid')
- response_potential: float32 [12288, 256], P(('grid', 'tile'))
Inputs may be any that keep to these rules, and one draw needn't show every extreme that they name: Each row names 2 different blocks of the window of 3 blocks around the batch's region. The live points of batch b are its first counts[b] slots; every device holds at least one full batch.
All inputs are finite; a program needn't handle non-finite values.
Results may differ from a plain program's by a relative error of at most 0.0061.
Values may be sent and summed in bfloat16 or wider, within the bound.
A program may use at most 128 MiB of HBM per device.

v0:
```python
import jax
import jax.numpy as jnp
from jax import lax
from jax.sharding import PartitionSpec as P


def with_halo(array, sides, width):
    for axis, dim in sides:
        size, length = (lax.axis_size(axis), array.shape[dim])
        up = [(i, (i + 1) % size) for i in range(size)]
        down = [(j, i) for i, j in up]
        last = lax.slice_in_dim(array, length - width, length, axis=dim)
        initial = lax.slice_in_dim(array, 0, width, axis=dim)
        before = lax.ppermute(last, axis, up)
        after = lax.ppermute(initial, axis, down)
        array = jnp.concatenate([before, array, after], axis=dim)
    return array


def copy_for_each(array, axis):
    size = lax.axis_size(axis)
    return lax.all_to_all(
        jnp.broadcast_to(array[None], (size, *array.shape)), axis, 0, 0, tiled=True
    )


def over_copies(array, axis):
    return copy_for_each(array, axis).sum(axis=0)


def window_rows(window, blocks, block_rows):
    stacked = window.reshape(-1, block_rows, window.shape[1])
    picked = jnp.take(stacked, blocks, axis=0)
    return picked.reshape(blocks.shape[0], -1, window.shape[1])


def per_device(
    basis_values,
    blocks,
    counts,
    weighted_potential,
    xc_kernel,
    occ_coef,
    virt_coef,
    occ_energy,
    virt_energy,
):
    nbatch, points, columns = basis_values.shape
    per_batch = blocks.shape[1]
    block_rows = columns // per_batch
    region_rows = occ_coef.shape[0]
    occ_count = occ_coef.shape[1]
    win_blocks = 3 * region_rows // block_rows
    live_mask = lax.broadcasted_iota(jnp.int32, (nbatch, points), 1) < counts[:, None]
    occ_window = with_halo(occ_coef, (("grid", 0),), region_rows)
    occ_rows = window_rows(occ_window, blocks, block_rows)
    occ_values = jnp.einsum(
        "bpk,bko->bpo", basis_values, occ_rows, preferred_element_type=jnp.float32
    )
    weights = jnp.where(live_mask, weighted_potential, 0.0)
    scaled = (weights[:, :, None] * occ_values).astype(jnp.bfloat16)
    contrib = jnp.einsum("bpk,bpo->bko", basis_values, scaled, preferred_element_type=jnp.float32)
    contrib = contrib.reshape(nbatch * per_batch, block_rows * occ_count)
    selector = (
        blocks.reshape(1, -1) == lax.broadcasted_iota(jnp.int32, (win_blocks, 1), 0)
    ).astype(jnp.float32)
    window_sums = jnp.dot(
        selector, contrib, precision=lax.Precision.HIGHEST, preferred_element_type=jnp.float32
    )
    window_sums = window_sums.reshape(3 * region_rows, occ_count)
    padded = with_halo(window_sums, (("grid", 0),), region_rows)
    own_part = (
        padded[:region_rows] + padded[2 * region_rows : 3 * region_rows] + padded[4 * region_rows :]
    )
    ham_occ = over_copies(own_part, "tile").astype(jnp.bfloat16)
    contract_rows = (((0,), (0,)), ((), ()))
    partial_ham = lax.dot_general(
        virt_coef, ham_occ, contract_rows, preferred_element_type=jnp.float32
    )
    virt_ham = lax.psum(partial_ham, "grid")
    rotation = (virt_ham / (occ_energy[None, :] - virt_energy[:, None])).astype(jnp.bfloat16)
    coef_part = jnp.dot(virt_coef, rotation, preferred_element_type=jnp.float32)
    response_coef = over_copies(coef_part, "tile").astype(jnp.bfloat16)
    coef_window = with_halo(response_coef, (("grid", 0),), region_rows)
    coef_rows = window_rows(coef_window, blocks, block_rows)
    resp_values = jnp.einsum(
        "bpk,bko->bpo", basis_values, coef_rows, preferred_element_type=jnp.float32
    )
    density = 4.0 * jnp.sum(occ_values * resp_values, axis=2)
    response_potential = jnp.where(live_mask, xc_kernel * density, 0.0)
    return (response_coef, response_potential)


def solution(mesh):
    in_specs = (
        P(("grid", "tile"), None, None),
        P(("grid", "tile"), None),
        P(("grid", "tile")),
        P(("grid", "tile"), None),
        P(("grid", "tile"), None),
        P("grid", None),
        P("grid", "tile"),
        P(),
        P("tile"),
    )
    out_specs = (P("grid", None), P(("grid", "tile"), None))
    return jax.shard_map(
        per_device, mesh=mesh, in_specs=in_specs, out_specs=out_specs, check_vma=False
    )
```

profile of v0, /device:TPU:1, one launch (start us, length us, event | category | flops | bytes accessed | tf_op | source)
XLA Modules:
  0.0 332.0 jit_solution(5822200128893390782)
XLA Ops:
  7.2 5.5 %collective-permute-start = (bf16[64,512]{1,0:T(8,128)(2,1)}, bf16[64,512]{1,0:T(8,128)(2,1)S(1)}, u32[]{:S(2)}, u32[]{:S(2)}) collective-permute-start(bf16[64,512]{1,0:T(8,128)(2,1)} %param.16), channel_id=1, source_target_pairs={{0,4},{4,8},{8,12},{12,16},{16,20},{20,24},{24,28},{28,32},{32,36}... | collective-permute-start | bytes 196616 | tf_op jit(solution)/shard_map/ppermute | solution.py:14
  12.7 5.3 %collective-permute-start.1 = (bf16[64,512]{1,0:T(8,128)(2,1)}, bf16[64,512]{1,0:T(8,128)(2,1)S(1)}, u32[]{:S(2)}, u32[]{:S(2)}) collective-permute-start(bf16[64,512]{1,0:T(8,128)(2,1)} %param.16), channel_id=1, source_target_pairs={{4,0},{8,4},{12,8},{16,12},{20,16},{24,20},{28,24},{32,28},{36,32}... | collective-permute-start | bytes 196616 | tf_op jit(solution)/shard_map/ppermute | solution.py:15
  18.0 0.7 compare_select_fusion
  18.7 0.7 compare_and_fusion
  19.4 0.8 copy.26
  20.4 0.1 copy.27
  20.6 0.8 fusion.6
  21.4 0.9 pad_maximum_fusion
  22.3 2.5 gather_fusion
  24.8 2.2 broadcast_select_fusion.1
  27.0 1.8 fusion.9
  28.9 4.6 %copy-done.1 = f32[24,512,256]{2,1,0:T(8,128)} copy-done((f32[24,512,256]{2,1,0:T(8,128)}, f32[24,512,256]{2,1,0:T(8,128)S(1)}, u32[]{:S(2)}) %copy-start.1) | copy-done | bytes 12582936
  33.4 4.4 %fusion.2 = f32[24,128,512]{1,2,0:T(8,128)} fusion(bf16[24,256,128]{2,1,0:T(8,128)(2,1)S(1)} %copy-done, f32[24,512,256]{2,1,0:T(8,128)S(1)} %fusion.9, f32[24,256]{1,0:T(8,128)S(1)} %fusion.6), kind=kOutput, calls=%fused_computation.10 | convolution fusion | flops 811597824 | bytes 20471808 | tf_op jit(solution)/shard_map/bpk,bpo->bko/dot_general | solution.py:62
  37.9 6.6 %copy.30 = f32[24,128,512]{2,1,0:T(8,128)} copy(f32[24,128,512]{1,2,0:T(8,128)} %fusion.2) | data formatting | bytes 12582912 | tf_op jit(solution)/shard_map/bpk,bpo->bko/dot_general | solution.py:62
  44.4 7.2 %reshape.38 = f32[48,32768]{1,0:T(8,128)} reshape(f32[24,128,512]{2,1,0:T(8,128)} %copy.30) | data formatting | bytes 12582912 | tf_op jit(solution)/shard_map/reshape | solution.py:63
  51.6 4.9 %fusion.7 = f32[3,32768]{1,0:T(4,128)S(1)} fusion(f32[48,32768]{1,0:T(8,128)} %reshape.38, s32[48]{0:T(128)S(1)} %eq.15), kind=kOutput, calls=%fused_computation.26 | convolution fusion | flops 56623248 | bytes 6684864 | tf_op jit(solution)/shard_map/dot_general | solution.py:67
  56.5 1.0 slice_reduce_fusion.1
  57.6 1.9 collective-permute-start.2
  59.5 7.9 %collective-permute-start.3 = (f32[64,512]{1,0:T(8,128)S(1)}, f32[64,512]{1,0:T(8,128)S(1)}, u32[]{:S(2)}, u32[]{:S(2)}) collective-permute-start(f32[64,512]{1,0:T(8,128)S(1)} %slice.23), channel_id=1, source_target_pairs={{4,0},{8,4},{12,8},{16,12},{20,16},{24,20},{28,24},{32,28},{36,32}... | collective-permute-start | bytes 393224 | tf_op jit(solution)/shard_map/ppermute | solution.py:15
  67.5 0.9 collective-permute-done.3
  68.5 10.7 %all_to_all.10 = f32[4,64,512]{2,1,0:T(8,128)S(1)} all-to-all(f32[4,64,512]{2,1,0:T(8,128)S(1)} %broadcast_in_dim.19), channel_id=1, replica_groups=mesh['grid'=128,'tile'=4] {'tile'}, dimensions={0} | all-to-all | bytes 1048576 | tf_op jit(solution)/shard_map/all_to_all | solution.py:22
  79.4 2.6 convolution_bitcast_fusion
  82.0 205.5 %all-reduce.2.cloned.1.call-done = f32[1920,512]{0,1:T(8,128)} async-done(((f32[1920,512]{0,1:T(8,128)}), f32[1920,512]{0,1:T(8,128)}) %all-reduce.2.cloned.1.call-update) | async-done | bytes 3932176 | tf_op jit(solution)/shard_map/psum | solution.py:80
  287.5 2.9 fusion.4
  290.4 11.7 %all_to_all.11 = f32[4,64,512]{2,1,0:T(8,128)S(1)} all-to-all(f32[4,64,512]{2,1,0:T(8,128)S(1)} %broadcast_in_dim.32), channel_id=1, replica_groups=mesh['grid'=128,'tile'=4] {'tile'}, dimensions={0} | all-to-all | bytes 1048576 | tf_op jit(solution)/shard_map/all_to_all | solution.py:22
  302.2 5.4 %collective-permute-start.4 = (bf16[64,512]{1,0:T(8,128)(2,1)S(1)}, bf16[64,512]{1,0:T(8,128)(2,1)S(1)}, u32[]{:S(2)}, u32[]{:S(2)}) collective-permute-start(bf16[64,512]{1,0:T(8,128)(2,1)S(1)} %reduce_sum.28), channel_id=1, source_target_pairs={{0,4},{4,8},{8,12},{12,16},{16,20},{20,24},{24,28},{28,32},{32,36}... | collective-permute-start | bytes 196616 | tf_op jit(solution)/shard_map/ppermute | solution.py:14
  307.6 2.1 collective-permute-start.5
  309.7 3.5 %collective-permute-done.5 = bf16[64,512]{1,0:T(8,128)(2,1)S(1)} collective-permute-done((bf16[64,512]{1,0:T(8,128)(2,1)S(1)}, bf16[64,512]{1,0:T(8,128)(2,1)S(1)}, u32[]{:S(2)}, u32[]{:S(2)}) %collective-permute-start.5) | collective-permute-done | bytes 65568 | tf_op jit(solution)/shard_map/ppermute | solution.py:15
  313.2 2.5 gather_fusion.1
  315.8 2.2 broadcast_select_fusion
  318.0 6.4 %multiply_reduce_fusion = f32[24,256]{1,0:T(8,128)S(1)} fusion(f32[24,512,256]{2,1,0:T(8,128)} %copy-done.1, bf16[24,128,512]{2,1,0:T(8,128)(2,1)S(1)} %bitcast.23, bf16[24,256,128]{2,1,0:T(8,128)(2,1)S(1)} %copy-done), kind=kOutput, calls=%fused_computation.2 | convolution fusion | flops 811591680 | bytes 17326080 | tf_op jit(solution)/shard_map/bpk,bko->bpo/dot_general | solution.py:86
  324.5 0.7 multiply_select_fusion
  (34 shorter events, 0.7 us)
Async XLA Ops:
  7.2 19.9 %copy-start = (bf16[24,256,128]{2,1,0:T(8,128)(2,1)S(1)}, bf16[24,256,128]{2,1,0:T(8,128)(2,1)}, u32[]{:S(2)}) copy-start(bf16[24,256,128]{2,1,0:T(8,128)(2,1)} %param.11) | copy-start | bytes 4718596
  7.2 280.3 %all-reduce.2.cloned.1.call-start = ((), (), s32[]{:S(2)}) async-start(), calls=%async_computation.2 | async-start | bytes 7864320 | tf_op jit(solution)/shard_map/psum | solution.py:80
  7.2 14.2 %collective-permute-start = (bf16[64,512]{1,0:T(8,128)(2,1)}, bf16[64,512]{1,0:T(8,128)(2,1)S(1)}, u32[]{:S(2)}, u32[]{:S(2)}) collective-permute-start(bf16[64,512]{1,0:T(8,128)(2,1)} %param.16), channel_id=1, source_target_pairs={{0,4},{4,8},{8,12},{12,16},{16,20},{20,24},{24,28},{28,32},{32,36}... | collective-permute-start | bytes 196616 | tf_op jit(solution)/shard_map/ppermute | solution.py:14
  12.7 8.6 %collective-permute-start.1 = (bf16[64,512]{1,0:T(8,128)(2,1)}, bf16[64,512]{1,0:T(8,128)(2,1)S(1)}, u32[]{:S(2)}, u32[]{:S(2)}) collective-permute-start(bf16[64,512]{1,0:T(8,128)(2,1)} %param.16), channel_id=1, source_target_pairs={{4,0},{8,4},{12,8},{16,12},{20,16},{24,20},{28,24},{32,28},{36,32}... | collective-permute-start | bytes 196616 | tf_op jit(solution)/shard_map/ppermute | solution.py:15
  28.9 4.6 %copy-start.1 = (f32[24,512,256]{2,1,0:T(8,128)}, f32[24,512,256]{2,1,0:T(8,128)S(1)}, u32[]{:S(2)}) copy-start(f32[24,512,256]{2,1,0:T(8,128)S(1)} %fusion.9) | copy-start | bytes 37748740
  56.5 22.8 %copy-start.3 = (bf16[64,1920]{1,0:T(8,128)(2,1)S(1)}, bf16[64,1920]{1,0:T(8,128)(2,1)}, u32[]{:S(2)}) copy-start(bf16[64,1920]{1,0:T(8,128)(2,1)} %param.17) | copy-start | bytes 737284
  57.6 9.9 %collective-permute-start.2 = (f32[64,512]{1,0:T(8,128)S(1)}, f32[64,512]{1,0:T(8,128)S(1)}, u32[]{:S(2)}, u32[]{:S(2)}) collective-permute-start(f32[64,512]{1,0:T(8,128)S(1)} %slice.19), channel_id=1, source_target_pairs={{0,4},{4,8},{8,12},{12,16},{16,20},{20,24},{24,28},{28,32},{32,36}... | collective-permute-start | bytes 393224 | tf_op jit(solution)/shard_map/ppermute | solution.py:14
  59.5 8.9 %collective-permute-start.3 = (f32[64,512]{1,0:T(8,128)S(1)}, f32[64,512]{1,0:T(8,128)S(1)}, u32[]{:S(2)}, u32[]{:S(2)}) collective-permute-start(f32[64,512]{1,0:T(8,128)S(1)} %slice.23), channel_id=1, source_target_pairs={{4,0},{8,4},{12,8},{16,12},{20,16},{24,20},{28,24},{32,28},{36,32}... | collective-permute-start | bytes 393224 | tf_op jit(solution)/shard_map/ppermute | solution.py:15
  79.3 208.1 %copy-start.6 = (f32[1920]{0:T(1024)S(1)}, f32[1920]{0:T(1024)}, u32[]{:S(2)}) copy-start(f32[1920]{0:T(1024)} %param.19) | copy-start | bytes 23044
  79.4 208.1 %copy-start.7 = (f32[512]{0:T(512)S(1)}, f32[512]{0:T(512)}, u32[]{:S(2)}) copy-start(f32[512]{0:T(512)} %param.18) | copy-start | bytes 6148
  302.2 13.6 %copy-start.2 = (bf16[64,512]{1,0:T(8,128)(2,1)}, bf16[64,512]{1,0:T(8,128)(2,1)S(1)}, u32[]{:S(2)}) copy-start(bf16[64,512]{1,0:T(8,128)(2,1)S(1)} %reduce_sum.28) | copy-start | bytes 196612
  302.2 7.5 %collective-permute-start.4 = (bf16[64,512]{1,0:T(8,128)(2,1)S(1)}, bf16[64,512]{1,0:T(8,128)(2,1)S(1)}, u32[]{:S(2)}, u32[]{:S(2)}) collective-permute-start(bf16[64,512]{1,0:T(8,128)(2,1)S(1)} %reduce_sum.28), channel_id=1, source_target_pairs={{0,4},{4,8},{8,12},{12,16},{16,20},{20,24},{24,28},{28,32},{32,36}... | collective-permute-start | bytes 196616 | tf_op jit(solution)/shard_map/ppermute | solution.py:14
  307.6 5.6 %collective-permute-start.5 = (bf16[64,512]{1,0:T(8,128)(2,1)S(1)}, bf16[64,512]{1,0:T(8,128)(2,1)S(1)}, u32[]{:S(2)}, u32[]{:S(2)}) collective-permute-start(bf16[64,512]{1,0:T(8,128)(2,1)S(1)} %reduce_sum.28), channel_id=1, source_target_pairs={{4,0},{8,4},{12,8},{16,12},{20,16},{24,20},{28,24},{32,28},{36,32}... | collective-permute-start | bytes 196616 | tf_op jit(solution)/shard_map/ppermute | solution.py:15
  318.0 6.5 %copy-start.4 = (f32[24,256]{1,0:T(8,128)S(1)}, f32[24,256]{1,0:T(8,128)}, u32[]{:S(2)}) copy-start(f32[24,256]{1,0:T(8,128)} %param.15) | copy-start | bytes 73732
  318.0 6.5 %copy-start.5 = (s32[24]{0:T(128)S(1)}, s32[24]{0:T(128)}, u32[]{:S(2)}) copy-start(s32[24]{0:T(128)} %param.13) | copy-start | bytes 292
Sparse Core Ops, SparseCore 0:
  82.1 205.3 all-reduce.1
where the time goes:
time: 333 us; the launch traced here: 332 us
  waiting for transfers between devices  210 us (63%)
  starting transfers between devices  28.2 us (8%)
  local copies, waits for them, and re-layouts  25.7 us (8%)
  matrix products  23.1 us (7%)
  blocking collectives  22.4 us (7%)
  between operations  14.3 us (4%)
  other arithmetic  8.31 us (2%)
    psum x1, waiting for transfers between devices, per_device(): virt_ham = lax.psum(partial_ham, 'grid')  206 us
    all_to_all x2, blocking collectives, copy_for_each(): lax.all_to_all(jnp.broadcast_to(array[None], (size, *array.shape)), axis,...  22.4 us
    ppermute x3, starting transfers between devices, with_halo(): after = lax.ppermute(initial, axis, down)  15.3 us
    ppermute x3, starting transfers between devices, with_halo(): before = lax.ppermute(last, axis, up)  12.8 us
    reshape x1, local copies, waits for them, and re-layouts, per_device(): contrib = contrib.reshape(nbatch * per_batch, block_rows * occ_count)  7.17 us
  transfers between devices with their start and end apart: 7, of which 3 were waited for; matrix products, arithmetic and copies ran while one was open for 1% of the time, Pallas kernels for 0%

commit v1 on v0

v1 whole, which is shorter than its diff:
```python
import functools

import jax
import jax.numpy as jnp
from jax import lax
from jax.experimental import pallas as pl
from jax.experimental.pallas import tpu as pltpu
from jax.sharding import PartitionSpec as P

MESH = pl.DeviceIdType.MESH
B16 = jnp.bfloat16
F32 = jnp.float32
HAM_LINK = jnp.bfloat16
VIRT_LINK = jnp.bfloat16
COEF_LINK = jnp.bfloat16
NT = (((1,), (1,)), ((), ()))
NN = (((1,), (0,)), ((), ()))
BLK = 64
WIN = 256
SL = 64


def dot(a, b, dims=NN):
    return lax.dot_general(a, b, dims, preferred_element_type=F32)


def split(a):
    high = a.astype(B16)
    return high, (a - high.astype(F32)).astype(B16)


def kernel(
    topo, basis, blocks, counts, wpot, xc, occ, virt, eocc, evirt,
    coef_out, pot_out,
    occw, occt, bw, mat, ps, rb, hz, v2, evb, eot, ws, wr, rz, cs, cr, cw,
    sa, ra, sv1, rv1, sv2, rv2, svf, rvf, sv3, rv3, se, re,
    sb, rbs, sh, rh, sw, rw, sr, rr, sc, rc, sd, rd,
):
    nx, ny, nz = topo
    nq = ny * nz
    wy = 4 * WIN // ny
    g = lax.axis_index("grid")
    t = lax.axis_index("tile")
    c = g % 2
    q = g // 2
    z = q % nz
    y = q // nz
    gother = (g + 2 * nq - 1 + 2 * c) % (2 * nq)
    qup = (q + 1) % nq
    qdown = (q + nq - 1) % nq
    qother = (q + nq - 1 + 2 * c) % nq
    s_me = t * 2 + c
    nbatch = basis.shape[0]
    pending = []

    def zring(d):
        zz = (z + d) % nz
        return zz, 2 * (y * nz + zz) + c

    def yring(d):
        yy = (y + d) % ny
        return yy, 2 * (yy * nz + z) + c

    def push(src, dst, send, recv, gg, tt):
        copy = pltpu.make_async_remote_copy(
            src_ref=src, dst_ref=dst, send_sem=send, recv_sem=recv,
            device_id=(gg, tt), device_id_type=MESH,
        )
        copy.start()
        pending.append(copy)

    def arrive(dst, send, recv, gg, tt):
        pltpu.make_async_remote_copy(
            src_ref=dst, dst_ref=dst, send_sem=send, recv_sem=recv,
            device_id=(gg, tt), device_id_type=MESH,
        ).wait_recv()

    def vstart(zz):
        return pl.multiple_of(WIN * zz - 128 * (zz // (nz - 1)), 128)

    bar = pltpu.get_barrier_semaphore()
    own_chip = [(dc, dt) for dc in range(2) for dt in range(nx) if (dc, dt) != (0, 0)]
    for dc, dt in own_chip:
        pl.semaphore_signal(
            bar, inc=1, device_id=(2 * q + (c + dc) % 2, (t + dt) % nx), device_id_type=MESH
        )
    for qq in (qup, qdown):
        for cc in range(2):
            for tt in range(nx):
                pl.semaphore_signal(bar, inc=1, device_id=(2 * qq + cc, tt), device_id_type=MESH)
    for d in range(1, nz):
        pl.semaphore_signal(bar, inc=1, device_id=(zring(d)[1], t), device_id_type=MESH)
    for d in range(1, ny):
        pl.semaphore_signal(bar, inc=1, device_id=(yring(d)[1], t), device_id_type=MESH)

    mat[...] = jnp.zeros_like(mat)
    occw[pl.ds(pl.multiple_of(BLK * c, BLK), BLK), :] = occ[...]
    occw[pl.ds(pl.multiple_of(128 + BLK * c, BLK), BLK), :] = jnp.zeros((BLK, 512), B16)
    v2[t, z, c] = virt[:, pl.ds(vstart(z), WIN)]
    evb[:, pl.ds(pl.multiple_of(WIN * t, WIN), WIN)] = jnp.broadcast_to(
        evirt[:, pl.ds(vstart(z), WIN)], (8, WIN)
    )
    eot[...] = jnp.transpose(jnp.broadcast_to(eocc[...], (128, 512)))

    pl.semaphore_wait(bar, len(own_chip) + 4 * nx + nz - 1 + ny - 1)

    own_rows = pl.ds(pl.multiple_of(BLK * c, BLK), BLK)
    far_rows = pl.ds(pl.multiple_of(128 + BLK * c, BLK), BLK)
    sib = 2 * q + 1 - c
    push(occ, occw.at[own_rows], sa.at[0], ra.at[0], sib, t)
    push(occ, occw.at[far_rows], sa.at[1], ra.at[1], gother, t)
    for d in range(1, nz):
        zz, gg = zring(d)
        push(virt.at[:, pl.ds(vstart(zz), WIN)], v2.at[t, z, c], sv1.at[d], rv1.at[d], gg, t)
    mine_e = evb.at[:, pl.ds(pl.multiple_of(WIN * t, WIN), WIN)]
    for d in range(1, nx):
        push(mine_e, mine_e, se.at[d], re.at[d], g, (t + d) % nx)

    row = lax.broadcasted_iota(jnp.int32, (WIN, 128), 0)
    col = lax.broadcasted_iota(jnp.int32, (WIN, 128), 1)
    lane = lax.broadcasted_iota(jnp.int32, (1, WIN), 1)

    def integrate(b, carry):
        first = (BLK * (blocks[0, b] + c + 3)) % WIN
        second = (BLK * (blocks[1, b] + c + 3)) % WIN
        target = jnp.where(col < BLK, col + first, col - BLK + second)
        pick = jnp.where(row == target, 1.0, 0.0).astype(B16)
        spread = dot(pick, basis[b], NT)
        wide = spread.astype(B16)
        bw[b] = wide
        weight = jnp.where(lane < counts[0, b], wpot[pl.ds(b, 1), :], 0.0)
        mat[...] += dot((spread * weight).astype(B16), wide, NT)
        return carry

    lax.fori_loop(0, nbatch, integrate, 0)

    arrive(occw.at[pl.ds(pl.multiple_of(BLK * (1 - c), BLK), BLK)], sa.at[0], ra.at[0], sib, t)
    arrive(occw.at[pl.ds(pl.multiple_of(192 - BLK * c, BLK), BLK)], sa.at[1], ra.at[1], gother, t)
    occt[...] = jnp.transpose(occw[...].astype(F32)).astype(B16)
    high, low = split(mat[...])
    part = dot(occt[...], high) + dot(occt[...], low)
    for s in range(2 * nx):
        for h in range(2):
            ps[s, h] = part[SL * s : SL * s + SL, 128 * h : 128 * h + 128].astype(HAM_LINK)

    slot = 4 * c + t
    rb[slot] = ps[s_me, 0]
    for n, (dc, dt) in enumerate(own_chip):
        cc, tt = (c + dc) % 2, (t + dt) % nx
        push(ps.at[tt * 2 + cc, 0], rb.at[slot], sb.at[n], rbs.at[slot], 2 * q + cc, tt)
    for cc in range(2):
        for tt in range(nx):
            push(ps.at[tt * 2 + cc, 1], rb.at[8 + slot], sb.at[8 + 4 * cc + tt], rbs.at[8 + slot],
                 2 * qother + cc, tt)

    for d in range(1, nz):
        zz = (z + nz - d) % nz
        arrive(v2.at[t, zz, c], sv1.at[d], rv1.at[d], zring(nz - d)[1], t)
    right, left = (t + 1) % nx, (t + nx - 1) % nx
    push(v2.at[t, :, c], v2.at[t, :, c], sv2.at[0], rv2.at[0], g, right)
    push(v2.at[t, :, c], v2.at[t, :, c], sv2.at[1], rv2.at[1], g, left)
    push(v2.at[t, :, c], v2.at[t, :, c], sv3.at[0], rv3.at[0], sib, t)

    for dc, dt in own_chip:
        cc, tt = (c + dc) % 2, (t + dt) % nx
        k = 4 * cc + tt
        arrive(rb.at[k], sb.at[0], rbs.at[k], 2 * q + cc, tt)
    for tt in range(nx):
        arrive(rb.at[8 + tt], sb.at[0], rbs.at[8 + tt], 2 * qup, tt)
        arrive(rb.at[12 + tt], sb.at[0], rbs.at[12 + tt], 2 * qdown + 1, tt)
    ham = rb[0].astype(F32)
    for k in range(1, 16):
        ham = ham + rb[k].astype(F32)
    zcols = lambda zz: pl.ds(pl.multiple_of(128 * zz, 128), 128)
    hz[:, zcols(z)] = ham.astype(B16)
    for d in range(1, nz):
        push(hz.at[:, zcols(z)], hz.at[:, zcols(z)], sh.at[d], rh.at[d], zring(d)[1], t)

    half = nz // 2
    arrive(v2.at[left, :, c], sv2.at[0], rv2.at[0], g, left)
    push(v2.at[left, 0:half, c], v2.at[left, 0:half, c], svf.at[0], rvf.at[0], g, right)
    push(v2.at[left, :, c], v2.at[left, :, c], sv3.at[1], rv3.at[1], sib, t)
    arrive(v2.at[right, :, c], sv2.at[1], rv2.at[1], g, right)
    push(v2.at[right, half:nz, c], v2.at[right, half:nz, c], svf.at[1], rvf.at[1], g, left)
    push(v2.at[right, :, c], v2.at[right, :, c], sv3.at[2], rv3.at[2], sib, t)
    across = (t + 2) % nx
    arrive(v2.at[across, 0:half, c], svf.at[0], rvf.at[0], g, left)
    arrive(v2.at[across, half:nz, c], svf.at[1], rvf.at[1], g, right)
    push(v2.at[across, :, c], v2.at[across, :, c], sv3.at[3], rv3.at[3], sib, t)
    for d in range(1, nz):
        arrive(hz.at[:, zcols((z + nz - d) % nz)], sh.at[d], rh.at[d], zring(nz - d)[1], t)
    for n, tt in enumerate((t, left, right, across)):
        arrive(v2.at[tt, :, 1 - c], sv3.at[n], rv3.at[n], sib, t)

    for tt in range(nx):
        part = dot(hz[...], v2[tt].reshape(nz * 128, WIN))
        for j in range(WIN // 128):
            at = 128 * (2 * tt + j)
            ws[at // wy, :, at % wy : at % wy + 128] = part[:, 128 * j : 128 * j + 128].astype(VIRT_LINK)
    wr[y] = ws[y]
    for d in range(1, ny):
        yy, gg = yring(d)
        push(ws.at[yy], wr.at[y], sw.at[d], rw.at[d], gg, t)
    for d in range(1, nx):
        tt = (t + nx - d) % nx
        theirs = evb.at[:, pl.ds(pl.multiple_of(WIN * tt, WIN), WIN)]
        arrive(theirs, se.at[d], re.at[d], g, tt)
    for d in range(1, ny):
        arrive(wr.at[(y + ny - d) % ny], sw.at[d], rw.at[d], yring(ny - d)[1], t)
    total = wr[0].astype(F32)
    for k in range(1, ny):
        total = total + wr[k].astype(F32)
    ycols = lambda yy: pl.ds(pl.multiple_of(wy * yy, 128), wy)
    gap = eot[pl.ds(pl.multiple_of(SL * s_me, SL), SL), 0:1] - evb[0:1, ycols(y)]
    place = lax.broadcasted_iota(jnp.int32, (SL, wy), 1) + wy * y
    repeat = jnp.logical_and(place % WIN < 128 * (z // (nz - 1)), place >= 0)
    rz[:, ycols(y)] = jnp.where(repeat, 0.0, total / gap).astype(B16)
    for d in range(1, ny):
        push(rz.at[:, ycols(y)], rz.at[:, ycols(y)], sr.at[d], rr.at[d], yring(d)[1], t)
    for d in range(1, ny):
        arrive(rz.at[:, ycols((y + ny - d) % ny)], sr.at[d], rr.at[d], yring(ny - d)[1], t)

    coef = dot(rz[:, 0:WIN], v2[0].reshape(nz * 128, WIN), NT)
    for tt in range(1, nx):
        coef += dot(rz[:, WIN * tt : WIN * tt + WIN], v2[tt].reshape(nz * 128, WIN), NT)
    for k in range(nz):
        cs[k] = coef[:, 128 * k : 128 * k + 128].astype(COEF_LINK)
    cr[z] = cs[z]
    for d in range(1, nz):
        zz, gg = zring(d)
        push(cs.at[zz], cr.at[z], sc.at[d], rc.at[d], gg, t)
    for d in range(1, nz):
        arrive(cr.at[(z + nz - d) % nz], sc.at[d], rc.at[d], zring(nz - d)[1], t)
    done = cr[0].astype(F32)
    for k in range(1, nz):
        done = done + cr[k].astype(F32)
    cw[0, s_me] = done.astype(B16)

    for n, (dc, dt) in enumerate(own_chip):
        push(cw.at[0, s_me], cw.at[0, s_me], sd.at[n], rd.at[0, s_me],
             2 * q + (c + dc) % 2, (t + dt) % nx)
    for tt in range(nx):
        push(cw.at[0, s_me], cw.at[1, s_me], sd.at[8 + tt], rd.at[1, s_me], 2 * qup, tt)
        push(cw.at[0, s_me], cw.at[1, s_me], sd.at[12 + tt], rd.at[1, s_me], 2 * qdown + 1, tt)
    for dc, dt in own_chip:
        cc, tt = (c + dc) % 2, (t + dt) % nx
        k = tt * 2 + cc
        arrive(cw.at[0, k], sd.at[0], rd.at[0, k], 2 * q + cc, tt)
    for cc in range(2):
        for tt in range(nx):
            k = tt * 2 + cc
            arrive(cw.at[1, k], sd.at[0], rd.at[1, k], 2 * qother + cc, tt)

    near = cw[0].reshape(512, 128)
    far = cw[1].reshape(512, 128)
    krow = lax.broadcasted_iota(jnp.int32, (BLK, 128), 0)
    kcol = lax.broadcasted_iota(jnp.int32, (BLK, 128), 1)
    pick = jnp.where(kcol == krow + BLK * c, 1.0, 0.0).astype(B16)
    coef_out[...] = dot(pick, near, NT).astype(B16)
    mat[:, 0:128] = dot(occw[...], near)
    mat[:, 128:256] = dot(occw[...], far)
    high, low = split(mat[...])
    bw_low = low
    occt_high = occt.at[0:WIN, :]
    occt_low = occt.at[WIN : 2 * WIN, :]
    occt_high[...] = high
    occt_low[...] = bw_low

    def respond(b, carry):
        wide = bw[b]
        resp = dot(occt_high[...], wide) + dot(occt_low[...], wide)
        density = 4.0 * jnp.sum(resp * wide.astype(F32), axis=0, keepdims=True)
        value = xc[pl.ds(b, 1), :] * density
        pot_out[pl.ds(b, 1), :] = jnp.where(lane < counts[0, b], value, 0.0)
        return carry

    lax.fori_loop(0, nbatch, respond, 0)
    for copy in pending:
        copy.wait_send()


def per_device(topo, basis, blocks, counts, wpot, xc, occ, virt, eocc, evirt):
    nx, ny, nz = topo
    nbatch, points, columns = basis.shape
    rows, nocc = occ.shape
    wy = 4 * WIN // ny
    vmem = pl.BlockSpec(memory_space=pltpu.VMEM)
    smem = pl.BlockSpec(memory_space=pltpu.SMEM)
    dma = pltpu.SemaphoreType.DMA
    scratch = [
        pltpu.VMEM((WIN, nocc), B16),
        pltpu.VMEM((nocc, WIN), B16),
        pltpu.VMEM((nbatch, WIN, points), B16),
        pltpu.VMEM((WIN, WIN), F32),
        pltpu.VMEM((8, 2, SL, 128), HAM_LINK),
        pltpu.VMEM((16, SL, 128), HAM_LINK),
        pltpu.VMEM((SL, 128 * nz), B16),
        pltpu.VMEM((nx, nz, 2, BLK, WIN), B16),
        pltpu.VMEM((8, nx * WIN), F32),
        pltpu.VMEM((nocc, 128), F32),
        pltpu.VMEM((ny, SL, wy), VIRT_LINK),
        pltpu.VMEM((ny, SL, wy), VIRT_LINK),
        pltpu.VMEM((SL, nx * WIN), B16),
        pltpu.VMEM((nz, SL, 128), COEF_LINK),
        pltpu.VMEM((nz, SL, 128), COEF_LINK),
        pltpu.VMEM((2, 8, SL, 128), B16),
        dma((2,)), dma((2,)),
        dma((nz,)), dma((nz,)),
        dma((2,)), dma((2,)),
        dma((2,)), dma((2,)),
        dma((4,)), dma((4,)),
        dma((nx,)), dma((nx,)),
        dma((16,)), dma((16,)),
        dma((nz,)), dma((nz,)),
        dma((ny,)), dma((ny,)),
        dma((ny,)), dma((ny,)),
        dma((nz,)), dma((nz,)),
        dma((16,)), dma((2, 8)),
    ]
    return pl.pallas_call(
        functools.partial(kernel, topo),
        out_shape=(
            jax.ShapeDtypeStruct((rows, nocc), B16),
            jax.ShapeDtypeStruct((nbatch, points), F32),
        ),
        in_specs=[vmem, smem, smem] + [vmem] * 6,
        out_specs=(vmem, vmem),
        scratch_shapes=scratch,
        compiler_params=pltpu.CompilerParams(collective_id=0, has_side_effects=True),
        name="dfpt_cycle",
    )(
        basis, blocks.T, counts.reshape(1, -1), wpot, xc, occ, virt,
        eocc.reshape(1, -1), evirt.reshape(1, -1),
    )


def solution(mesh):
    side = 1
    while 2 * side * side < mesh.shape["grid"]:
        side += 1
    topo = (mesh.shape["tile"], side, side)
    in_specs = (
        P(("grid", "tile"), None, None),
        P(("grid", "tile"), None),
        P(("grid", "tile")),
        P(("grid", "tile"), None),
        P(("grid", "tile"), None),
        P("grid", None),
        P("grid", "tile"),
        P(),
        P("tile"),
    )
    out_specs = (P("grid", None), P(("grid", "tile"), None))
    return jax.shard_map(
        functools.partial(per_device, topo),
        mesh=mesh, in_specs=in_specs, out_specs=out_specs, check_vma=False,
    )
```

time: 333 us -> 80.6 us (0.24)
  waiting for transfers between devices: 210 us -> 0 us
  Pallas kernels: 0 us -> 75.5 us
  starting transfers between devices: 28.2 us -> 0 us
  matrix products: 23.1 us -> 0 us
  blocking collectives: 22.4 us -> 0 us
  local copies, waits for them, and re-layouts: 25.7 us -> 4.12 us
  between operations: 14.3 us -> 0.64 us
  other arithmetic: 8.31 us -> 0 us
    psum x1 -> x0, waiting for transfers between devices: 206 us -> none  [per_device(): virt_ham = lax.psum(partial_ham, 'grid')]
    pallas_call x0 -> x1, Pallas kernels: none -> 75.5 us  [per_device(): pl.pallas_call(functools.partial(kernel, topo), out_shape=(jax.ShapeDtype...]
    ppermute x6 -> x0, starting transfers between devices: 28.2 us -> none  [the longest x3 15.3 us: with_halo(): after = lax.ppermute(initial, axis, down)]
    dot_general x6 -> x0, matrix products: 23.1 us -> none  [the longest x1 6.45 us: per_device(): jnp.einsum('bpk,bko->bpo', basis_values, coef_rows, preferred_element_typ...]
    all_to_all x2 -> x0, blocking collectives: 22.4 us -> none  [copy_for_each(): lax.all_to_all(jnp.broadcast_to(array[None], (size, *array.shape)), axis,...]
    select_n x5 -> x0, other arithmetic: 6.64 us -> none  [the longest x3 5.15 us: window_rows(): picked = jnp.take(stacked, blocks, axis=0)]
    dot_general x1 -> x0, local copies, waits for them, and re-layouts: 6.58 us -> none  [per_device(): jnp.einsum('bpk,bpo->bko', basis_values, scaled, preferred_element_type=j...]
    reshape x1, local copies, waits for them, and re-layouts: 7.17 us -> 1.3 us  [per_device(): evirt.reshape(1, -1)]
  transfers between devices with their start and end apart: 7 -> 0, of which waited for: 3 -> 0; matrix products, arithmetic and copies ran while one was open for 1% -> 0% of each run, Pallas kernels for 0% -> 0%
where the time goes in v1:
time: 80.6 us; the launch traced here: 80.3 us
  Pallas kernels  75.5 us (94%)
  local copies, waits for them, and re-layouts  4.12 us (5%)
    pallas_call x1, Pallas kernels, per_device(): pl.pallas_call(functools.partial(kernel, topo), out_shape=(jax.ShapeDtype...  75.5 us
    unnamed x2, local copies, waits for them, and re-layouts  2.82 us

profile of v1, /device:TPU:1, one launch (start us, length us, event | category | flops | bytes accessed | tf_op | source)
XLA Modules:
  0.0 80.3 jit_solution(10688024170632696175)
XLA Ops:
  0.6 1.3 %reshape.15.evirt = f32[1,1920]{1,0:T(1,128)} reshape(f32[1920]{0:T(1024)} %param.17) | data formatting | bytes 15360 | tf_op jit(solution)/shard_map/reshape | solution.py:333
  1.9 75.5 %dfpt_cycle.1 = (bf16[64,512]{1,0:T(8,128)(2,1)}, f32[24,256]{1,0:T(8,128)}) custom-call(bf16[24,256,128]{2,1,0:T(8,128)(2,1)} %basis.1, s32[2,24]{1,0:T(2,128)} %bitcast.4, s32[1,24]{1,0:T(1,128)} %bitcast.5, f32[24,256]{1,0:T(8,128)} %wpot.1, f32[24,256]{1,0:T(8,128)} %xc.1, bf16[64,512]{1,0:T(8,128)(2,1)} %occ.1, bf16[64,1920]{1,0:T(8,128)(2,1)} %virt.1, ...), custom_call_target="tpu_custom_call" | custom-call | tf_op jit(solution)/shard_map/dfpt_cycle/pallas_call | solution.py:320
  77.4 1.5 %copy.13 = bf16[64,512]{1,0:T(8,128)(2,1)} copy(bf16[64,512]{1,0:T(8,128)(2,1)} %get-tuple-element.4) | data formatting | bytes 131072
  78.9 1.3 %copy.14 = f32[24,256]{1,0:T(8,128)} copy(f32[24,256]{1,0:T(8,128)} %get-tuple-element.5) | data formatting | bytes 49152

commit v2 on v1

v2 whole, which is shorter than its diff:
```python
import functools

import jax
import jax.numpy as jnp
from jax import lax
from jax.experimental import pallas as pl
from jax.experimental.pallas import tpu as pltpu
from jax.sharding import PartitionSpec as P

MESH = pl.DeviceIdType.MESH
B16 = jnp.bfloat16
F32 = jnp.float32
HAM_LINK = jnp.bfloat16
VIRT_LINK = jnp.bfloat16
COEF_LINK = jnp.bfloat16
NT = (((1,), (1,)), ((), ()))
NN = (((1,), (0,)), ((), ()))
BLK = 64
WIN = 256
SL = 64
PER = 4


def dot(a, b, dims=NN):
    return lax.dot_general(a, b, dims, preferred_element_type=F32)


def split(a):
    high = a.astype(B16)
    return high, (a - high.astype(F32)).astype(B16)


def kernel(
    topo, basis_in, blocks_in, counts_in, wpot_in, occ, virt, eocc_in, evirt_in,
    coef_out, dens_out,
    blocks, counts, basis, wpot, eocc, evirt, coef, dens, gmat,
    occw, occt, bw, mat, ps, rb, hz, v2, evb, eot, ws, wr, rz, cs, cr, cw,
    sl, sa, ra, sv1, rv1, sv2, rv2, svf, rvf, sv3, rv3, se, re,
    sb, rbs, sh, rh, sw, rw, sr, rr, sc, rc, sd, rd,
):
    nx, ny, nz = topo
    nq = ny * nz
    wy = 4 * WIN // ny
    g = lax.axis_index("grid")
    t = lax.axis_index("tile")
    c = g % 2
    q = g // 2
    z = q % nz
    y = q // nz
    gother = (g + 2 * nq - 1 + 2 * c) % (2 * nq)
    qup = (q + 1) % nq
    qdown = (q + nq - 1) % nq
    qother = (q + nq - 1 + 2 * c) % nq
    s_me = t * 2 + c
    groups, _, span = bw.shape
    per = span // WIN
    nbatch = groups * per
    third = nbatch // 3

    def local(src, dst, sem):
        copy = pltpu.make_async_copy(src, dst, sem)
        copy.start()
        return copy

    def zring(d):
        zz = (z + d) % nz
        return zz, 2 * (y * nz + zz) + c

    def yring(d):
        yy = (y + d) % ny
        return yy, 2 * (yy * nz + z) + c

    def push(src, dst, send, recv, gg, tt):
        pltpu.make_async_remote_copy(
            src_ref=src, dst_ref=dst, send_sem=send, recv_sem=recv,
            device_id=(gg, tt), device_id_type=MESH,
        ).start()

    def bytes_of(ref, sem):
        pltpu.make_async_copy(ref, ref, sem).wait()

    def vstart(zz):
        return pl.multiple_of(WIN * zz - 128 * (zz // (nz - 1)), 128)

    def outward(n):
        return sorted(range(1, n), key=lambda d: (min(d, n - d), d))

    znear, ynear = outward(nz), outward(ny)
    zfar, yfar = znear[::-1], ynear[::-1]
    xnear = [0] + outward(nx)
    xfar = xnear[::-1]

    bar = pltpu.get_barrier_semaphore()
    own_chip = [(dc, dt) for dc in range(2) for dt in range(nx) if (dc, dt) != (0, 0)]
    for dc, dt in own_chip:
        pl.semaphore_signal(
            bar, inc=1, device_id=(2 * q + (c + dc) % 2, (t + dt) % nx), device_id_type=MESH
        )
    for qq in (qup, qdown):
        for cc in range(2):
            for tt in range(nx):
                pl.semaphore_signal(bar, inc=1, device_id=(2 * qq + cc, tt), device_id_type=MESH)
    for d in range(1, nz):
        pl.semaphore_signal(bar, inc=1, device_id=(zring(d)[1], t), device_id_type=MESH)
    for d in range(1, ny):
        pl.semaphore_signal(bar, inc=1, device_id=(yring(d)[1], t), device_id_type=MESH)

    own_rows = pl.ds(pl.multiple_of(BLK * c, BLK), BLK)
    far_rows = pl.ds(pl.multiple_of(128 + BLK * c, BLK), BLK)
    load_b = local(blocks_in, blocks, sl.at[8])
    load_n = local(counts_in, counts, sl.at[9])
    load_w = local(wpot_in, wpot, sl.at[3])
    loads = [
        local(basis_in.at[pl.ds(third * k, third)], basis.at[pl.ds(third * k, third)], sl.at[k])
        for k in range(3)
    ]
    load_o = local(occ, occw.at[own_rows], sl.at[5])
    load_v = local(virt.at[:, pl.ds(vstart(z), WIN)], v2.at[t, z, c], sl.at[4])
    load_eo = local(eocc_in, eocc, sl.at[6])
    load_ev = local(evirt_in, evirt, sl.at[7])
    mat[...] = jnp.zeros_like(mat)
    occw[far_rows, :] = jnp.zeros((BLK, occw.shape[1]), B16)

    pl.semaphore_wait(bar, len(own_chip) + 4 * nx + nz - 1 + ny - 1)

    sib = 2 * q + 1 - c
    push(occ, occw.at[far_rows], sa, ra.at[1], gother, t)
    push(occ, occw.at[own_rows], sa, ra.at[0], sib, t)
    for n, d in enumerate(znear, 1):
        zz, gg = zring(d)
        push(virt.at[:, pl.ds(vstart(zz), WIN)], v2.at[t, z, c], sv1, rv1.at[(n + 1) // 2], gg, t)
    right, left, across = (t + 1) % nx, (t + nx - 1) % nx, (t + 2) % nx
    load_v.wait()
    push(v2.at[t, z, c], v2.at[t, z, c], sv2.at[0], rv2.at[0, 0], g, right)
    push(v2.at[t, z, c], v2.at[t, z, c], sv2.at[1], rv2.at[1, 0], g, left)

    row = lax.broadcasted_iota(jnp.int32, (WIN, 128), 0)
    col = lax.broadcasted_iota(jnp.int32, (WIN, 128), 1)
    lane = lax.broadcasted_iota(jnp.int32, (1, WIN), 1)
    load_w.wait()
    load_b.wait()
    load_n.wait()

    def integrate(n, carry):
        wides, scaled = [], []
        for j in range(per):
            b = per * n + j
            first = (BLK * (blocks[0, b] + c + 3)) % WIN
            second = (BLK * (blocks[1, b] + c + 3)) % WIN
            target = jnp.where(col < BLK, col + first, col - BLK + second)
            pick = jnp.where(row == target, 1.0, 0.0).astype(B16)
            spread = dot(pick, basis[b], NT)
            wide = spread.astype(B16)
            bw[n, :, WIN * j : WIN * j + WIN] = wide
            weight = jnp.where(lane < counts[0, b], wpot[pl.ds(b, 1), :], 0.0)
            wides.append(wide)
            scaled.append((spread * weight).astype(B16))
        mat[...] += dot(jnp.concatenate(scaled, axis=1), jnp.concatenate(wides, axis=1), NT)
        return carry

    for k in range(3):
        loads[k].wait()
        lax.fori_loop(groups * k // 3, groups * (k + 1) // 3, integrate, 0)

    load_o.wait()
    bytes_of(occw.at[pl.ds(pl.multiple_of(BLK * (1 - c), BLK), BLK)], ra.at[0])
    bytes_of(occw.at[pl.ds(pl.multiple_of(192 - BLK * c, BLK), BLK)], ra.at[1])
    occt[...] = jnp.transpose(occw[...].astype(F32)).astype(B16)
    high, low = split(mat[...])
    part = dot(occt[...], high) + dot(occt[...], low)
    for s in range(2 * nx):
        for h in range(2):
            ps[s, h] = part[SL * s : SL * s + SL, 128 * h : 128 * h + 128].astype(HAM_LINK)

    slot = 4 * c + t
    rb[slot] = ps[s_me, 0]
    for dt in xfar:
        tt = (t + dt) % nx
        for cc in range(2):
            push(ps.at[tt * 2 + cc, 1], rb.at[8 + slot], sb, rbs,
                 2 * qother + cc, tt)
        for dc in range(2):
            if dc or dt:
                cc = (c + dc) % 2
                push(ps.at[tt * 2 + cc, 0], rb.at[slot], sb, rbs,
                     2 * q + cc, tt)

    load_eo.wait()
    load_ev.wait()
    eot[...] = jnp.transpose(jnp.broadcast_to(eocc[...], (128, eocc.shape[1])))
    evb[:, pl.ds(pl.multiple_of(WIN * t, WIN), WIN)] = jnp.broadcast_to(
        evirt[pl.ds(vstart(z), WIN)].reshape(1, WIN), (8, WIN)
    )
    mine_e = evb.at[:, pl.ds(pl.multiple_of(WIN * t, WIN), WIN)]
    for d in range(1, nx):
        push(mine_e, mine_e, se, re, g, (t + d) % nx)

    order = [0] + znear
    steps = [order[0:1]] + [order[n : n + 2] for n in range(1, nz, 2)]
    for n, ds in enumerate(steps):
        if n:
            bytes_of(v2.at[t, 0 : len(ds), c], rv1.at[n])
            for d in ds:
                mine = v2.at[t, (z + d) % nz, c]
                push(mine, mine, sv2.at[0], rv2.at[0, n], g, right)
                push(mine, mine, sv2.at[1], rv2.at[1, n], g, left)
    push(v2.at[t, :, c], v2.at[t, :, c], sv3, rv3, sib, t)

    bytes_of(rb.at[0:15], rbs)
    ham = rb[0].astype(F32)
    for k in range(1, 16):
        ham = ham + rb[k].astype(F32)
    zcols = lambda zz: pl.ds(pl.multiple_of(128 * zz, 128), 128)
    hz[:, zcols(z)] = ham.astype(B16)
    for d in zfar:
        push(hz.at[:, zcols(z)], hz.at[:, zcols(z)], sh, rh, zring(d)[1], t)

    for n, ds in enumerate(steps):
        for k, (frm, to) in enumerate(((left, right), (right, left))):
            bytes_of(v2.at[frm, 0 : len(ds), c], rv2.at[k, n])
            for m, d in enumerate(ds):
                if (m + (n > 0) * (len(ds) == 1)) % 2 == k:
                    theirs = v2.at[frm, (z + d) % nz, c]
                    push(theirs, theirs, svf, rvf, g, to)
    push(v2.at[left, :, c], v2.at[left, :, c], sv3, rv3, sib, t)
    push(v2.at[right, :, c], v2.at[right, :, c], sv3, rv3, sib, t)
    bytes_of(v2.at[across, :, c], rvf)
    push(v2.at[across, :, c], v2.at[across, :, c], sv3, rv3, sib, t)
    bytes_of(hz.at[:, 0 : 128 * (nz - 1)], rh)
    bytes_of(v2.at[:, :, 1 - c], rv3)

    for tt in range(nx):
        part = dot(hz[...], v2[tt].reshape(nz * 128, WIN))
        for j in range(WIN // 128):
            at = 128 * (2 * tt + j)
            ws[at // wy, :, at % wy : at % wy + 128] = part[:, 128 * j : 128 * j + 128].astype(VIRT_LINK)
    wr[y] = ws[y]
    for d in yfar:
        yy, gg = yring(d)
        push(ws.at[yy], wr.at[y], sw, rw, gg, t)
    bytes_of(evb.at[:, 0 : WIN * (nx - 1)], re)
    bytes_of(wr.at[0 : ny - 1], rw)
    total = wr[0].astype(F32)
    for k in range(1, ny):
        total = total + wr[k].astype(F32)
    ycols = lambda yy: pl.ds(pl.multiple_of(wy * yy, 128), wy)
    gap = eot[pl.ds(pl.multiple_of(SL * s_me, SL), SL), 0:1] - evb[0:1, ycols(y)]
    place = lax.broadcasted_iota(jnp.int32, (SL, wy), 1) + wy * y
    repeat = place % WIN < 128 * (z // (nz - 1))
    rz[:, ycols(y)] = jnp.where(repeat, 0.0, total / gap).astype(B16)
    for d in yfar:
        push(rz.at[:, ycols(y)], rz.at[:, ycols(y)], sr, rr, yring(d)[1], t)
    bytes_of(rz.at[:, 0 : wy * (ny - 1)], rr)

    part = dot(rz[:, 0:WIN], v2[0].reshape(nz * 128, WIN), NT)
    for tt in range(1, nx):
        part += dot(rz[:, WIN * tt : WIN * tt + WIN], v2[tt].reshape(nz * 128, WIN), NT)
    for k in range(nz):
        cs[k] = part[:, 128 * k : 128 * k + 128].astype(COEF_LINK)
    cr[z] = cs[z]
    for d in zfar:
        zz, gg = zring(d)
        push(cs.at[zz], cr.at[z], sc, rc, gg, t)
    bytes_of(cr.at[0 : nz - 1], rc)
    done = cr[0].astype(F32)
    for k in range(1, nz):
        done = done + cr[k].astype(F32)
    cw[0, s_me] = done.astype(B16)

    for dt in xfar:
        tt = (t + dt) % nx
        push(cw.at[0, s_me], cw.at[1, s_me], sd, rd.at[1], 2 * qup, tt)
        push(cw.at[0, s_me], cw.at[1, s_me], sd, rd.at[1], 2 * qdown + 1, tt)
        for dc in range(2):
            if dc or dt:
                push(cw.at[0, s_me], cw.at[0, s_me], sd, rd.at[0],
                     2 * q + (c + dc) % 2, tt)
    bytes_of(cw.at[0, 0:7], rd.at[0])
    near = cw[0].reshape(8 * SL, 128)
    krow = lax.broadcasted_iota(jnp.int32, (BLK, 128), 0)
    kcol = lax.broadcasted_iota(jnp.int32, (BLK, 128), 1)
    pick = jnp.where(kcol == krow + BLK * c, 1.0, 0.0).astype(B16)
    coef[...] = dot(pick, near, NT)
    give_c = local(coef, coef_out, sl.at[0])
    gmat[:, 0:128] = dot(occw[...], near).astype(B16)
    bytes_of(cw.at[1], rd.at[1])
    far = cw[1].reshape(8 * SL, 128)
    gmat[:, 128:256] = dot(occw[...], far).astype(B16)

    def respond(n, carry):
        wide = bw[n]
        resp = dot(gmat[...], wide)
        total = jnp.sum(resp * wide.astype(F32), axis=0, keepdims=True)
        for j in range(per):
            dens[pl.ds(per * n + j, 1), :] = 4.0 * total[:, WIN * j : WIN * j + WIN]
        return carry

    lax.fori_loop(0, groups, respond, 0)
    give_d = local(dens, dens_out, sl.at[1])
    bytes_of(occw.at[0:128], sa)
    bytes_of(v2.at[0, 0 : nz - 1, 0], sv1)
    bytes_of(v2.at[0, :, 0], sv2.at[0])
    bytes_of(v2.at[0, :, 0], sv2.at[1])
    bytes_of(v2.at[0, :, 0], svf)
    bytes_of(v2.at[:, :, 0], sv3)
    bytes_of(evb.at[:, 0 : WIN * (nx - 1)], se)
    bytes_of(rb.at[0:15], sb)
    bytes_of(hz.at[:, 0 : 128 * (nz - 1)], sh)
    bytes_of(ws.at[0 : ny - 1], sw)
    bytes_of(rz.at[:, 0 : wy * (ny - 1)], sr)
    bytes_of(cs.at[0 : nz - 1], sc)
    bytes_of(rb.at[0:15], sd)
    give_c.wait()
    give_d.wait()


def per_device(topo, basis, blocks, counts, wpot, xc, occ, virt, eocc, evirt):
    nx, ny, nz = topo
    nbatch, points, columns = basis.shape
    rows, nocc = occ.shape
    wy = 4 * WIN // ny
    per = PER
    hbm = pl.BlockSpec(memory_space=pl.ANY)
    dma = pltpu.SemaphoreType.DMA
    scratch = [
        pltpu.SMEM((2, nbatch), jnp.int32),
        pltpu.SMEM((1, nbatch), jnp.int32),
        pltpu.VMEM(basis.shape, B16),
        pltpu.VMEM(wpot.shape, F32),
        pltpu.VMEM((1, nocc), F32),
        pltpu.VMEM(evirt.shape, F32),
        pltpu.VMEM((rows, nocc), F32),
        pltpu.VMEM((nbatch, points), F32),
        pltpu.VMEM((WIN, WIN), B16),
        pltpu.VMEM((WIN, nocc), B16),
        pltpu.VMEM((nocc, WIN), B16),
        pltpu.VMEM((nbatch // per, WIN, per * points), B16),
        pltpu.VMEM((WIN, WIN), F32),
        pltpu.VMEM((8, 2, SL, 128), HAM_LINK),
        pltpu.VMEM((16, SL, 128), HAM_LINK),
        pltpu.VMEM((SL, 128 * nz), B16),
        pltpu.VMEM((nx, nz, 2, BLK, WIN), B16),
        pltpu.VMEM((8, nx * WIN), F32),
        pltpu.VMEM((nocc, 128), F32),
        pltpu.VMEM((ny, SL, wy), VIRT_LINK),
        pltpu.VMEM((ny, SL, wy), VIRT_LINK),
        pltpu.VMEM((SL, nx * WIN), B16),
        pltpu.VMEM((nz, SL, 128), COEF_LINK),
        pltpu.VMEM((nz, SL, 128), COEF_LINK),
        pltpu.VMEM((2, 8, SL, 128), B16),
        dma((10,)),
        dma, dma((2,)),
        dma, dma((nz // 2 + 1,)),
        dma((2,)), dma((2, nz // 2 + 1)),
        dma, dma,
        dma, dma,
        dma, dma,
        dma, dma,
        dma, dma,
        dma, dma,
        dma, dma,
        dma, dma,
        dma, dma((2,)),
    ]
    coef, density = pl.pallas_call(
        functools.partial(kernel, topo),
        out_shape=(
            jax.ShapeDtypeStruct((rows, nocc), F32),
            jax.ShapeDtypeStruct((nbatch, points), F32),
        ),
        in_specs=[hbm] * 8,
        out_specs=(hbm, hbm),
        scratch_shapes=scratch,
        compiler_params=pltpu.CompilerParams(collective_id=0, has_side_effects=True),
        name="dfpt_cycle",
    )(basis, blocks.T, counts.reshape(1, -1), wpot, occ, virt, eocc.reshape(1, -1), evirt)
    live = lax.broadcasted_iota(jnp.int32, (nbatch, points), 1) < counts[:, None]
    return coef.astype(B16), jnp.where(live, xc * density, 0.0)


def solution(mesh):
    side = 1
    while 2 * side * side < mesh.shape["grid"]:
        side += 1
    topo = (mesh.shape["tile"], side, side)
    in_specs = (
        P(("grid", "tile"), None, None),
        P(("grid", "tile"), None),
        P(("grid", "tile")),
        P(("grid", "tile"), None),
        P(("grid", "tile"), None),
        P("grid", None),
        P("grid", "tile"),
        P(),
        P("tile"),
    )
    out_specs = (P("grid", None), P(("grid", "tile"), None))
    return jax.shard_map(
        functools.partial(per_device, topo),
        mesh=mesh, in_specs=in_specs, out_specs=out_specs, check_vma=False,
    )
```

time: 80.6 us -> 65.1 us (0.81)
  Pallas kernels: 75.5 us -> 61.2 us
  local copies, waits for them, and re-layouts: 4.12 us -> 0.01 us
  other arithmetic: 0 us -> 2.96 us
    pallas_call x1, Pallas kernels: 75.5 us -> 61.2 us  [per_device(): pl.pallas_call(functools.partial(kernel, topo), out_shape=(jax.ShapeDtype...]
    unnamed x2 -> x4, local copies, waits for them, and re-layouts: 2.82 us -> 0.01 us
    convert_element_type x0 -> x1, other arithmetic: none -> 1.54 us  [per_device(): return (coef.astype(B16), jnp.where(live, xc * density, 0.0))]
    select_n x0 -> x1, other arithmetic: none -> 1.42 us  [per_device(): return (coef.astype(B16), jnp.where(live, xc * density, 0.0))]
    reshape x1 -> x0, local copies, waits for them, and re-layouts: 1.3 us -> none  [per_device(): evirt.reshape(1, -1)]
where the time goes in v2:
time: 65.1 us; the launch traced here: 64.9 us
  Pallas kernels  61.2 us (94%)
  other arithmetic  2.96 us (5%)
  between operations  0.66 us (1%)
    pallas_call x1, Pallas kernels, per_device(): pl.pallas_call(functools.partial(kernel, topo), out_shape=(jax.ShapeDtype...  61.2 us
    convert_element_type x1, other arithmetic, per_device(): return (coef.astype(B16), jnp.where(live, xc * density, 0.0))  1.54 us
    select_n x1, other arithmetic, per_device(): return (coef.astype(B16), jnp.where(live, xc * density, 0.0))  1.42 us

profile of v2, /device:TPU:1, one launch (start us, length us, event | category | flops | bytes accessed | tf_op | source)
XLA Modules:
  0.0 64.9 jit_solution(5418838090339501452)
XLA Ops:
  0.6 0.0 copy-start.1
  0.6 0.0 copy-start
  0.7 61.2 %dfpt_cycle.1 = (f32[64,512]{1,0:T(8,128)}, f32[24,256]{1,0:T(8,128)}) custom-call(bf16[24,256,128]{2,1,0:T(8,128)(2,1)} %basis_in.1, s32[2,24]{1,0:T(2,128)} %bitcast.5, s32[1,24]{1,0:T(1,128)} %bitcast.4, f32[24,256]{1,0:T(8,128)} %wpot_in.1, bf16[64,512]{1,0:T(8,128)(2,1)} %occ.1, bf16[64,1920]{1,0:T(8,128)(2,1)} %virt.1, f32[1,512]{1,0:T(1,128)} %bitcast.3, ...), custom_call_target="tpu_custom_call" | custom-call | tf_op jit(solution)/shard_map/dfpt_cycle/pallas_call | solution.py:365
  61.9 1.5 %convert_element_type.3 = bf16[64,512]{1,0:T(8,128)(2,1)} convert(f32[64,512]{1,0:T(8,128)} %get-tuple-element.4) | non-fusion elementwise | flops 32768 | bytes 196608 | tf_op jit(solution)/shard_map/convert_element_type | solution.py:378
  63.5 0.0 copy-done.1
  63.5 0.0 copy-done
  63.5 1.4 %multiply_select_fusion = f32[24,256]{1,0:T(8,128)} fusion(f32[24,256]{1,0:T(8,128)S(1)} %copy-done, f32[24,256]{1,0:T(8,128)} %get-tuple-element.5, s32[24]{0:T(128)S(1)} %copy-done.1), kind=kLoop, calls=%fused_computation | loop fusion | flops 18432 | bytes 73824 | tf_op jit(solution)/shard_map/jit(_where)/select_n | solution.py:378
Async XLA Ops:
  0.6 62.8 %copy-start.1 = (s32[24]{0:T(128)S(1)}, s32[24]{0:T(128)}, u32[]{:S(2)}) copy-start(s32[24]{0:T(128)} %param.11) | copy-start | bytes 292
  0.6 62.8 %copy-start = (f32[24,256]{1,0:T(8,128)S(1)}, f32[24,256]{1,0:T(8,128)}, u32[]{:S(2)}) copy-start(f32[24,256]{1,0:T(8,128)} %param.13) | copy-start | bytes 73732

commit v3 on v2

v3 whole, which is shorter than its diff:
```python
import functools

import jax
import jax.numpy as jnp
from jax import lax
from jax.experimental import pallas as pl
from jax.experimental.pallas import tpu as pltpu
from jax.sharding import PartitionSpec as P

MESH = pl.DeviceIdType.MESH
B16 = jnp.bfloat16
F32 = jnp.float32
HAM_LINK = jnp.bfloat16
VIRT_LINK = jnp.bfloat16
COEF_LINK = jnp.bfloat16
NT = (((1,), (1,)), ((), ()))
NN = (((1,), (0,)), ((), ()))
BLK = 64
WIN = 256
SL = 64
PER = 8
TALL = 192


def dot(a, b, dims=NN):
    return lax.dot_general(a, b, dims, preferred_element_type=F32)


def split(a):
    high = a.astype(B16)
    return high, (a - high.astype(F32)).astype(B16)


def kernel(
    topo, basis_in, blocks_in, counts_in, wpot_in, xc_in, occ, virt, eocc_in, evirt_in,
    coef_out, dens_out,
    blocks, counts, basis, wpot, xc, eocc, evirt, coef, dens, gmat,
    occw, occt, bw, mat, ps, po, rb, ro, hz, v2, evb, eot, ws, wr, rz, cs, cr, cw, cf, cp, staged,
    sl, sa, ra, sv1, rv1, sv2, rv2, svf, rvf, sv3, rv3, se, re,
    sb, rbs, sh, rh, sw, rw, sr, rr, sc, rc, sd, rd, ss, rs,
):
    nx, ny, nz = topo
    nq = ny * nz
    g = lax.axis_index("grid")
    t = lax.axis_index("tile")
    c = g % 2
    q = g // 2
    z = q % nz
    y = q // nz
    gother = (g + 2 * nq - 1 + 2 * c) % (2 * nq)
    qup = (q + 1) % nq
    qdown = (q + nq - 1) % nq
    qother = (q + nq - 1 + 2 * c) % nq
    s_me = t * 2 + c
    groups, _, span = bw.shape
    per = span // WIN
    nbatch = groups * per
    third = nbatch // 3

    def local(src, dst, sem):
        copy = pltpu.make_async_copy(src, dst, sem)
        copy.start()
        return copy

    def zring(d):
        zz = (z + d) % nz
        return zz, 2 * (y * nz + zz) + c

    def yring(d):
        yy = (y + d) % ny
        return yy, 2 * (yy * nz + z) + c

    def push(src, dst, send, recv, gg, tt):
        pltpu.make_async_remote_copy(
            src_ref=src, dst_ref=dst, send_sem=send, recv_sem=recv,
            device_id=(gg, tt), device_id_type=MESH,
        ).start()

    def bytes_of(ref, sem):
        pltpu.make_async_copy(ref, ref, sem).wait()

    def vstart(zz):
        return pl.multiple_of(WIN * zz - 128 * (zz // (nz - 1)), 128)

    def outward(n):
        return sorted(range(1, n), key=lambda d: (min(d, n - d), d))

    znear, ynear = outward(nz), outward(ny)
    zfar, yfar = znear[::-1], ynear[::-1]
    xnear = [0] + outward(nx)
    xfar = xnear[::-1]

    bar = pltpu.get_barrier_semaphore()
    own_chip = [(dc, dt) for dc in range(2) for dt in range(nx) if (dc, dt) != (0, 0)]
    for dc, dt in own_chip:
        pl.semaphore_signal(
            bar, inc=1, device_id=(2 * q + (c + dc) % 2, (t + dt) % nx), device_id_type=MESH
        )
    for qq in (qup, qdown):
        for cc in range(2):
            for tt in range(nx):
                pl.semaphore_signal(bar, inc=1, device_id=(2 * qq + cc, tt), device_id_type=MESH)
    for d in range(1, nz):
        pl.semaphore_signal(bar, inc=1, device_id=(zring(d)[1], t), device_id_type=MESH)
    for d in range(1, ny):
        pl.semaphore_signal(bar, inc=1, device_id=(yring(d)[1], t), device_id_type=MESH)

    own_rows = pl.ds(pl.multiple_of(BLK * c, BLK), BLK)
    far_rows = slice(2 * BLK, 3 * BLK)
    loads = [
        local(basis_in.at[pl.ds(third * k, third)], basis.at[pl.ds(third * k, third)], sl.at[k])
        for k in range(3)
    ]
    load_b = local(blocks_in, blocks, sl.at[8])
    load_n = local(counts_in, counts, sl.at[9])
    load_w = local(wpot_in, wpot, sl.at[3])
    load_v = local(virt.at[:, pl.ds(vstart(z), WIN)], v2.at[t, z, c], sl.at[4])

    pl.semaphore_wait(bar, len(own_chip) + 4 * nx + nz - 1 + ny - 1)

    sib = 2 * q + 1 - c
    push(occ, occw.at[far_rows], sa, ra.at[1], gother, t)
    push(occ, occw.at[own_rows], sa, ra.at[0], sib, t)
    right, left, across = (t + 1) % nx, (t + nx - 1) % nx, (t + 2) % nx
    steps = [[0], [1], [nz - 1]] + [znear[n : n + 2] for n in range(2, nz - 1, 2)]
    group_of = {d: n for n, ds in enumerate(steps) for d in ds}
    before = zring(nz - 1)
    chunk = virt.at[:, pl.ds(vstart(before[0]), WIN)]
    for k, to in enumerate((right, left)):
        push(chunk, staged.at[t], sv2.at[k], rv2.at[k, 1], g, to)
    for d in [1] + znear[2:] + [nz - 1]:
        zz, gg = zring(d)
        group = group_of[nz - d]
        push(virt.at[:, pl.ds(vstart(zz), WIN)], v2.at[t, z, c], sv1, rv1.at[group], gg, t)
    load_o = local(occ, occw.at[own_rows], sl.at[5])
    load_eo = local(eocc_in, eocc, sl.at[6])
    load_ev = local(evirt_in, evirt, sl.at[7])
    load_x = local(xc_in, xc, sl.at[10])
    mat[...] = jnp.zeros_like(mat)
    occw[3 * BLK : WIN, :] = jnp.zeros((BLK, occw.shape[1]), B16)

    row = lax.broadcasted_iota(jnp.int32, (TALL, 128), 0)
    col = lax.broadcasted_iota(jnp.int32, (TALL, 128), 1)
    lane = lax.broadcasted_iota(jnp.int32, (1, WIN), 1)
    load_w.wait()
    load_b.wait()
    load_n.wait()

    def integrate(n, carry):
        wides, scaled = [], []
        for j in range(per):
            b = per * n + j
            first = (BLK * (blocks[0, b] + c + 2)) % (3 * BLK)
            second = (BLK * (blocks[1, b] + c + 2)) % (3 * BLK)
            target = jnp.where(col < BLK, col + first, col - BLK + second)
            pick = jnp.where(row == target, 1.0, 0.0).astype(B16)
            spread = dot(pick, basis[b], NT)
            wide = spread.astype(B16)
            bw[n, :, WIN * j : WIN * j + WIN] = wide
            weight = jnp.where(lane < counts[0, b], wpot[pl.ds(b, 1), :], 0.0)
            wides.append(wide)
            scaled.append((spread * weight).astype(B16))
        mat[0:TALL, 0:TALL] += dot(jnp.concatenate(scaled, axis=1), jnp.concatenate(wides, axis=1), NT)
        return carry

    for k in range(3):
        loads[k].wait()
        lax.fori_loop(groups * k // 3, groups * (k + 1) // 3, integrate, 0)
        if k == 0:
            load_v.wait()
            for n, to in enumerate((right, left)):
                push(v2.at[t, z, c], v2.at[t, z, c], sv2.at[n], rv2.at[n, 0], g, to)

    load_o.wait()
    bytes_of(occw.at[pl.ds(pl.multiple_of(BLK * (1 - c), BLK), BLK)], ra.at[0])
    bytes_of(occw.at[far_rows], ra.at[1])
    occt[...] = jnp.transpose(occw[...].astype(F32)).astype(B16)
    high, low = split(mat[...])
    part = dot(occt[...], high) + dot(occt[...], low)
    half_lane = lax.broadcasted_iota(jnp.int32, (SL // 2, 128), 1) < BLK
    for s in range(2 * nx):
        rows = part[SL * s : SL * s + SL]
        ps[s] = rows[:, 0:128].astype(HAM_LINK)
        top, bottom = rows[0 : SL // 2, 128:256], rows[SL // 2 : SL, 128:256]
        po[s] = jnp.where(half_lane, top, pltpu.roll(bottom, BLK, 1)).astype(HAM_LINK)


    def along_x(n):
        ds = steps[n]
        bytes_of(v2.at[t, 0 : len(ds), c], rv1.at[n])
        for d in ds:
            mine = v2.at[t, (z + d) % nz, c]
            push(mine, mine, sv2.at[0], rv2.at[0, n], g, right)
            push(mine, mine, sv2.at[1], rv2.at[1, n], g, left)

    slot = 4 * c + t
    rb[slot] = ps[s_me]

    def give_ham():
        for dt in xfar:
            tt = (t + dt) % nx
            for cc in range(2):
                push(po.at[tt * 2 + cc], ro.at[slot], sb.at[1], rbs.at[1], 2 * qother + cc, tt)
            for dc in range(2):
                if dc or dt:
                    cc = (c + dc) % 2
                    push(ps.at[tt * 2 + cc], rb.at[slot], sb.at[0], rbs.at[0], 2 * q + cc, tt)

    give_ham()
    for k, (frm, to) in enumerate(((left, right), (right, left))):
        bytes_of(staged.at[0], rv2.at[k, 1])
        if k == 1:
            push(staged.at[frm], staged.at[frm], svf, rvf.at[0], g, to)
        push(staged.at[frm], v2.at[frm, z, c], ss, rs.at[k], before[1], t)
    for n in range(2, len(steps) - 1):
        along_x(n)
    bytes_of(staged.at[0], rvf.at[0])
    push(staged.at[across], v2.at[across, z, c], ss, rs.at[2], before[1], t)
    load_eo.wait()
    load_x.wait()
    load_ev.wait()
    eot[...] = jnp.transpose(jnp.broadcast_to(eocc[...], (128, eocc.shape[1])))
    evb[:, pl.ds(pl.multiple_of(WIN * t, WIN), WIN)] = jnp.broadcast_to(
        evirt[pl.ds(vstart(z), WIN)].reshape(1, WIN), (8, WIN)
    )
    mine_e = evb.at[:, pl.ds(pl.multiple_of(WIN * t, WIN), WIN)]
    for d in range(1, nx):
        push(mine_e, mine_e, se, re, g, (t + d) % nx)

    bytes_of(rb.at[0:7], rbs.at[0])
    bytes_of(ro, rbs.at[1])
    ham = rb[0].astype(F32)
    for k in range(1, 8):
        ham = ham + rb[k].astype(F32)
    above = ro[0].astype(F32)
    below = ro[4].astype(F32)
    for k in range(1, 4):
        above = above + ro[k].astype(F32)
        below = below + ro[4 + k].astype(F32)
    halo = jnp.concatenate([
        jnp.where(half_lane, below, pltpu.roll(above, BLK, 1)),
        jnp.where(half_lane, pltpu.roll(below, BLK, 1), above),
    ], axis=0)
    ham = ham + halo
    zcols = lambda zz: pl.ds(pl.multiple_of(128 * zz, 128), 128)
    hz[:, zcols(z)] = ham.astype(B16)
    for d in zfar:
        push(hz.at[:, zcols(z)], hz.at[:, zcols(z)], sh, rh, zring(d)[1], t)
    along_x(len(steps) - 1)
    bytes_of(v2.at[t, 0, c], rv1.at[1])
    push(v2.at[t, :, c], v2.at[t, :, c], sv3, rv3.at[0], sib, t)

    def to_sibling(tt, n, ds):
        for d in ds:
            block = v2.at[tt, (z + d) % nz, c]
            push(block, block, sv3, rv3.at[n], sib, t)

    rightward = (0, nz - 2)
    for n, ds in enumerate(steps):
        if n == 1:
            continue
        for k, (frm, to) in enumerate(((left, right), (right, left))):
            bytes_of(v2.at[frm, 0 : len(ds), c], rv2.at[k, n])
            for d in ds:
                if (d in rightward) == (k == 0):
                    theirs = v2.at[frm, (z + d) % nz, c]
                    push(theirs, theirs, svf, rvf.at[2 if n == len(steps) - 1 else 1], g, to)
            to_sibling(frm, 1 + k, ds)
    for k, frm in enumerate((left, right)):
        bytes_of(v2.at[frm, 0, c], rs.at[k])
        to_sibling(frm, 1 + k, [1])
    bytes_of(hz.at[:, 0 : 128 * (nz - 1)], rh)

    share = 8 // ny

    def virtual(tt, n):
        bytes_of(v2.at[tt, :, 1 - c], rv3.at[n])
        part = dot(hz[...], v2[tt].reshape(nz * 128, WIN))
        for k in range(8):
            i, a = 16 * (k // 2), 128 * (k % 2)
            ws[n, k] = part[i : i + 16, a : a + 128].astype(VIRT_LINK)
        wr[n, y] = ws[n, pl.ds(y * share, share)]
        for d in yfar:
            yy, gg = yring(d)
            push(ws.at[n, pl.ds(yy * share, share)], wr.at[n, y], sw, rw.at[n], gg, t)

    def rotate(tt, n):
        bytes_of(wr.at[n, 0 : ny - 1], rw.at[n])
        for h in range(share):
            k = y * share + h
            total = wr[n, 0, h].astype(F32)
            for yy in range(1, ny):
                total = total + wr[n, yy, h].astype(F32)
            i = pl.multiple_of(SL * s_me + 16 * (k // 2), 16)
            a = pl.multiple_of(WIN * tt + 128 * (k % 2), 128)
            gap = eot[pl.ds(i, 16), 0:1] - evb[0:1, pl.ds(a, 128)]
            repeat = lax.broadcasted_iota(jnp.int32, (16, 128), 1) * 0 + k % 2 < z // (nz - 1)
            rz[n, k] = jnp.where(repeat, 0.0, total / gap).astype(B16)
        mine = rz.at[n, pl.ds(y * share, share)]
        for d in yfar:
            push(mine, mine, sr, rr.at[n], yring(d)[1], t)

    def respond_to(tt, n):
        bytes_of(rz.at[n, 0 : (ny - 1) * share], rr.at[n])
        turn = jnp.concatenate([
            jnp.concatenate([rz[n, k], rz[n, k + 1]], axis=1) for k in range(0, 8, 2)
        ], axis=0)
        return dot(turn, v2[tt].reshape(nz * 128, WIN), NT)

    virtual(t, 0)
    last = steps[-1]
    bytes_of(v2.at[across, 0, c], rs.at[2])
    bytes_of(v2.at[across, 0 : nz - 1 - len(last), c], rvf.at[1])
    to_sibling(across, 3, [d for d in range(nz) if d not in last])
    virtual(left, 1)
    bytes_of(v2.at[across, 0 : len(last), c], rvf.at[2])
    to_sibling(across, 3, last)
    virtual(right, 2)
    virtual(across, 3)
    bytes_of(evb.at[:, 0 : WIN * (nx - 1)], re)
    tiles = (t, left, right, across)
    for n in range(nx - 1):
        rotate(tiles[n], n)
    rotate(tiles[nx - 1], nx - 1)
    part = respond_to(tiles[0], 0)
    for n in range(1, nx - 1):
        part += respond_to(tiles[n], n)
    part += respond_to(tiles[nx - 1], nx - 1)
    for k in range(nz):
        cs[k] = part[:, 128 * k : 128 * k + 128].astype(COEF_LINK)
    cr[z] = cs[z]
    for d in zfar:
        zz, gg = zring(d)
        push(cs.at[zz], cr.at[z], sc, rc, gg, t)
    bytes_of(cr.at[0 : nz - 1], rc)
    done = cr[0].astype(F32)
    for k in range(1, nz):
        done = done + cr[k].astype(F32)
    cw[s_me] = done.astype(B16)
    top, bottom = done[0 : SL // 2], done[SL // 2 : SL]
    cp[0] = jnp.where(half_lane, pltpu.roll(top, BLK, 1), bottom).astype(B16)
    cp[1] = jnp.where(half_lane, top, pltpu.roll(bottom, BLK, 1)).astype(B16)

    for dt in xfar:
        tt = (t + dt) % nx
        push(cp.at[0], cf.at[s_me], sd.at[1], rd.at[1], 2 * qup, tt)
        push(cp.at[1], cf.at[s_me], sd.at[1], rd.at[1], 2 * qdown + 1, tt)
        for dc in range(2):
            if dc or dt:
                push(cw.at[s_me], cw.at[s_me], sd.at[0], rd.at[0], 2 * q + (c + dc) % 2, tt)
    bytes_of(cw.at[0:7], rd.at[0])
    near = cw[...].reshape(8 * SL, 128)
    krow = lax.broadcasted_iota(jnp.int32, (BLK, 128), 0)
    kcol = lax.broadcasted_iota(jnp.int32, (BLK, 128), 1)
    pick = jnp.where(kcol == krow + BLK * c, 1.0, 0.0).astype(B16)
    coef[...] = dot(pick, near, NT).astype(B16)
    give_c = local(coef, coef_out, sl.at[0])
    gmat[:, 0:128] = dot(occw[...], near).astype(B16)
    bytes_of(cf, rd.at[1])
    pieces = []
    for k in range(8):
        packed = cf[k]
        pieces += [packed, pltpu.roll(packed.astype(F32), BLK, 1).astype(B16)]
    far = jnp.concatenate(pieces, axis=0)
    gmat[:, 128:256] = dot(occw[...], far).astype(B16)

    def respond(n, carry):
        wide = bw[n]
        resp = dot(gmat[0:TALL, 0:TALL], wide)
        total = jnp.sum(resp * wide.astype(F32), axis=0, keepdims=True)
        for j in range(per):
            b = per * n + j
            value = xc[pl.ds(b, 1), :] * (4.0 * total[:, WIN * j : WIN * j + WIN])
            dens[pl.ds(b, 1), :] = jnp.where(lane < counts[0, b], value, 0.0)
        return carry

    lax.fori_loop(0, groups, respond, 0)
    give_d = local(dens, dens_out, sl.at[1])
    bytes_of(occw.at[0:128], sa)
    bytes_of(v2.at[0, 0 : nz - 1, 0], sv1)
    bytes_of(v2.at[0, :, 0], sv2.at[0])
    bytes_of(v2.at[0, :, 0], sv2.at[1])
    bytes_of(v2.at[0, :, 0], svf)
    bytes_of(v2.at[0:3, 0, 0], ss)
    bytes_of(v2.at[:, :, 0], sv3)
    bytes_of(evb.at[:, 0 : WIN * (nx - 1)], se)
    bytes_of(rb.at[0:7], sb.at[0])
    bytes_of(ro, sb.at[1])
    bytes_of(hz.at[:, 0 : 128 * (nz - 1)], sh)
    bytes_of(wr.at[:, 0 : ny - 1], sw)
    bytes_of(rz.at[:, 0 : (ny - 1) * share], sr)
    bytes_of(cs.at[0 : nz - 1], sc)
    bytes_of(cw.at[0:7], sd.at[0])
    bytes_of(cf, sd.at[1])
    give_c.wait()
    give_d.wait()


def per_device(topo, basis, blocks, counts, wpot, xc, occ, virt, eocc, evirt):
    nx, ny, nz = topo
    nbatch, points, columns = basis.shape
    rows, nocc = occ.shape
    per = PER
    anywhere = pl.BlockSpec(memory_space=pl.ANY)
    dma = pltpu.SemaphoreType.DMA
    scratch = [
        pltpu.SMEM((2, nbatch), jnp.int32),
        pltpu.SMEM((1, nbatch), jnp.int32),
        pltpu.VMEM(basis.shape, B16),
        pltpu.VMEM(wpot.shape, F32),
        pltpu.VMEM(xc.shape, F32),
        pltpu.VMEM((1, nocc), F32),
        pltpu.VMEM(evirt.shape, F32),
        pltpu.VMEM((rows, nocc), B16),
        pltpu.VMEM((nbatch, points), F32),
        pltpu.VMEM((WIN, WIN), B16),
        pltpu.VMEM((WIN, nocc), B16),
        pltpu.VMEM((nocc, WIN), B16),
        pltpu.VMEM((nbatch // per, TALL, per * points), B16),
        pltpu.VMEM((WIN, WIN), F32),
        pltpu.VMEM((8, SL, 128), HAM_LINK),
        pltpu.VMEM((8, SL // 2, 128), HAM_LINK),
        pltpu.VMEM((8, SL, 128), HAM_LINK),
        pltpu.VMEM((8, SL // 2, 128), HAM_LINK),
        pltpu.VMEM((SL, 128 * nz), B16),
        pltpu.VMEM((nx, nz, 2, BLK, WIN), B16),
        pltpu.VMEM((8, nx * WIN), F32),
        pltpu.VMEM((nocc, 128), F32),
        pltpu.VMEM((nx, 8, 16, 128), VIRT_LINK),
        pltpu.VMEM((nx, ny, 8 // ny, 16, 128), VIRT_LINK),
        pltpu.VMEM((nx, 8, 16, 128), B16),
        pltpu.VMEM((nz, SL, 128), COEF_LINK),
        pltpu.VMEM((nz, SL, 128), COEF_LINK),
        pltpu.VMEM((8, SL, 128), B16),
        pltpu.VMEM((8, SL // 2, 128), B16),
        pltpu.VMEM((2, SL // 2, 128), B16),
        pltpu.VMEM((nx, BLK, WIN), B16),
        dma((11,)),
        dma, dma((2,)),
        dma, dma((nz // 2 + 2,)),
        dma((2,)), dma((2, nz // 2 + 2)),
        dma, dma((3,)),
        dma, dma((4,)),
        dma, dma,
        dma((2,)), dma((2,)),
        dma, dma,
        dma, dma((4,)),
        dma, dma((4,)),
        dma, dma,
        dma((2,)), dma((2,)),
        dma, dma((3,)),
    ]
    coef, potential = pl.pallas_call(
        functools.partial(kernel, topo),
        out_shape=(
            jax.ShapeDtypeStruct((rows, nocc), B16),
            jax.ShapeDtypeStruct((nbatch, points), F32),
        ),
        in_specs=[pl.BlockSpec(memory_space=pltpu.HBM)] * 9,
        out_specs=(anywhere, anywhere),
        scratch_shapes=scratch,
        compiler_params=pltpu.CompilerParams(collective_id=0, has_side_effects=True, vmem_limit_bytes=24 << 20),
        name="dfpt_cycle",
    )(*(
        pltpu.with_memory_space_constraint(array, pltpu.HBM)
        for array in (
            basis, blocks.T, counts.reshape(1, -1), wpot, xc, occ, virt,
            eocc.reshape(1, -1), evirt,
        )
    ))
    return pl.pallas_call(
        hand_out,
        out_shape=(
            jax.ShapeDtypeStruct(coef.shape, coef.dtype),
            jax.ShapeDtypeStruct(potential.shape, potential.dtype),
        ),
        in_specs=[anywhere] * 2,
        out_specs=(anywhere, anywhere),
        scratch_shapes=[dma((2,))],
        compiler_params=pltpu.CompilerParams(vmem_limit_bytes=1 << 20),
        name="hand_out",
    )(coef, potential)


def hand_out(coef, potential, coef_out, potential_out, sems):
    first = pltpu.make_async_copy(coef, coef_out, sems.at[0])
    second = pltpu.make_async_copy(potential, potential_out, sems.at[1])
    first.start()
    second.start()
    first.wait()
    second.wait()


def solution(mesh):
    side = 1
    while 2 * side * side < mesh.shape["grid"]:
        side += 1
    topo = (mesh.shape["tile"], side, side)
    in_specs = (
        P(("grid", "tile"), None, None),
        P(("grid", "tile"), None),
        P(("grid", "tile")),
        P(("grid", "tile"), None),
        P(("grid", "tile"), None),
        P("grid", None),
        P("grid", "tile"),
        P(),
        P("tile"),
    )
    out_specs = (P("grid", None), P(("grid", "tile"), None))
    return jax.shard_map(
        functools.partial(per_device, topo),
        mesh=mesh, in_specs=in_specs, out_specs=out_specs, check_vma=False,
    )
```

time: 65.1 us -> 57.5 us (0.88)
  Pallas kernels: 61.2 us -> 56.7 us
  other arithmetic: 2.96 us -> 0 us
    pallas_call x1, Pallas kernels: 61.2 us -> 56.1 us  [per_device(): pl.pallas_call(functools.partial(kernel, topo), out_shape=(jax.ShapeDtype...]
    convert_element_type x1 -> x0, other arithmetic: 1.54 us -> none  [per_device(): return (coef.astype(B16), jnp.where(live, xc * density, 0.0))]
    select_n x1 -> x0, other arithmetic: 1.42 us -> none  [per_device(): return (coef.astype(B16), jnp.where(live, xc * density, 0.0))]
    pallas_call x0 -> x1, Pallas kernels: none -> 0.65 us  [per_device(): pl.pallas_call(hand_out, out_shape=(jax.ShapeDtypeStruct(coef.shape, coef...]
where the time goes in v3:
time: 57.5 us; the launch traced here: 57.4 us
  Pallas kernels  56.7 us (99%)
  between operations  0.64 us (1%)
    pallas_call x1, Pallas kernels, per_device(): pl.pallas_call(functools.partial(kernel, topo), out_shape=(jax.ShapeDtype...  56.1 us

profile of v3, /device:TPU:1, one launch (start us, length us, event | category | flops | bytes accessed | tf_op | source)
XLA Modules:
  0.0 57.4 jit_solution(8856925567709692063)
XLA Ops:
  0.6 56.1 %dfpt_cycle.1 = (bf16[64,512]{1,0:T(8,128)(2,1)S(1)}, f32[24,256]{1,0:T(8,128)S(1)}) custom-call(bf16[24,256,128]{2,1,0:T(8,128)(2,1)} %basis_in.1, s32[2,24]{1,0:T(2,128)} %bitcast.4, s32[1,24]{1,0:T(1,128)} %bitcast.5, f32[24,256]{1,0:T(8,128)} %wpot_in.1, f32[24,256]{1,0:T(8,128)} %xc_in.1, bf16[64,512]{1,0:T(8,128)(2,1)} %occ.1, bf16[64,1920]{1,0:T(8,128)(2,1)} %virt.1, ...), custom_call_target="tpu_custom_call" | custom-call | tf_op jit(solution)/shard_map/dfpt_cycle/pallas_call | solution.py:453
  56.7 0.7 %hand_out.1 = (bf16[64,512]{1,0:T(8,128)(2,1)}, f32[24,256]{1,0:T(8,128)}) custom-call(bf16[64,512]{1,0:T(8,128)(2,1)S(1)} %get-tuple-element.4.coef, f32[24,256]{1,0:T(8,128)S(1)} %get-tuple-element.5.potential), custom_call_target="tpu_custom_call" | custom-call | tf_op jit(solution)/shard_map/hand_out/pallas_call | solution.py:471

commit v4 on v3

--- a/solution.py
+++ b/solution.py
@@ -19,6 +19,7 @@
 WIN = 256
 SL = 64
 PER = 8
+HALVES = 1
 TALL = 192
 
 
@@ -32,10 +33,10 @@
 
 
 def kernel(
-    topo, basis_in, blocks_in, counts_in, wpot_in, xc_in, occ, virt, eocc_in, evirt_in,
+    topo, basis_in, blocks_in, counts_in, wpot_in, xc_in, occ, virt_in, eocc_in, evirt_in,
     coef_out, dens_out,
     blocks, counts, basis, wpot, xc, eocc, evirt, coef, dens, gmat,
-    occw, occt, bw, mat, ps, po, rb, ro, hz, v2, evb, eot, ws, wr, rz, cs, cr, cw, cf, cp, staged,
+    occw, occt, bw, mat, ps, po, rb, ro, hz, v2, evb, eot, ws, wr, rz, cs, cr, cw, cf, cp, staged, virt,
     sl, sa, ra, sv1, rv1, sv2, rv2, svf, rvf, sv3, rv3, se, re,
     sb, rbs, sh, rh, sw, rw, sr, rr, sc, rc, sd, rd, ss, rs,
 ):
@@ -107,6 +108,8 @@
 
     own_rows = pl.ds(pl.multiple_of(BLK * c, BLK), BLK)
     far_rows = slice(2 * BLK, 3 * BLK)
+    load_o = local(occ, occw.at[own_rows], sl.at[5])
+    load_u = local(virt_in, virt, sl.at[11])
     loads = [
         local(basis_in.at[pl.ds(third * k, third)], basis.at[pl.ds(third * k, third)], sl.at[k])
         for k in range(3)
@@ -114,13 +117,15 @@
     load_b = local(blocks_in, blocks, sl.at[8])
     load_n = local(counts_in, counts, sl.at[9])
     load_w = local(wpot_in, wpot, sl.at[3])
-    load_v = local(virt.at[:, pl.ds(vstart(z), WIN)], v2.at[t, z, c], sl.at[4])
+    load_v = local(virt_in.at[:, pl.ds(vstart(z), WIN)], v2.at[t, z, c], sl.at[4])
 
     pl.semaphore_wait(bar, len(own_chip) + 4 * nx + nz - 1 + ny - 1)
 
     sib = 2 * q + 1 - c
-    push(occ, occw.at[far_rows], sa, ra.at[1], gother, t)
-    push(occ, occw.at[own_rows], sa, ra.at[0], sib, t)
+    load_o.wait()
+    push(occw.at[own_rows], occw.at[far_rows], sa, ra.at[1], gother, t)
+    push(occw.at[own_rows], occw.at[own_rows], sa, ra.at[0], sib, t)
+    load_u.wait()
     right, left, across = (t + 1) % nx, (t + nx - 1) % nx, (t + 2) % nx
     steps = [[0], [1], [nz - 1]] + [znear[n : n + 2] for n in range(2, nz - 1, 2)]
     group_of = {d: n for n, ds in enumerate(steps) for d in ds}
@@ -128,11 +133,10 @@
     chunk = virt.at[:, pl.ds(vstart(before[0]), WIN)]
     for k, to in enumerate((right, left)):
         push(chunk, staged.at[t], sv2.at[k], rv2.at[k, 1], g, to)
-    for d in [1] + znear[2:] + [nz - 1]:
+    for d in [nz // 2, 1] + znear[2:-1] + [nz - 1]:
         zz, gg = zring(d)
         group = group_of[nz - d]
         push(virt.at[:, pl.ds(vstart(zz), WIN)], v2.at[t, z, c], sv1, rv1.at[group], gg, t)
-    load_o = local(occ, occw.at[own_rows], sl.at[5])
     load_eo = local(eocc_in, eocc, sl.at[6])
     load_ev = local(evirt_in, evirt, sl.at[7])
     load_x = local(xc_in, xc, sl.at[10])
@@ -171,7 +175,6 @@
             for n, to in enumerate((right, left)):
                 push(v2.at[t, z, c], v2.at[t, z, c], sv2.at[n], rv2.at[n, 0], g, to)
 
-    load_o.wait()
     bytes_of(occw.at[pl.ds(pl.multiple_of(BLK * (1 - c), BLK), BLK)], ra.at[0])
     bytes_of(occw.at[far_rows], ra.at[1])
     occt[...] = jnp.transpose(occw[...].astype(F32)).astype(B16)
@@ -212,7 +215,7 @@
         if k == 1:
             push(staged.at[frm], staged.at[frm], svf, rvf.at[0], g, to)
         push(staged.at[frm], v2.at[frm, z, c], ss, rs.at[k], before[1], t)
-    for n in range(2, len(steps) - 1):
+    for n in range(2, len(steps)):
         along_x(n)
     bytes_of(staged.at[0], rvf.at[0])
     push(staged.at[across], v2.at[across, z, c], ss, rs.at[2], before[1], t)
@@ -246,7 +249,6 @@
     hz[:, zcols(z)] = ham.astype(B16)
     for d in zfar:
         push(hz.at[:, zcols(z)], hz.at[:, zcols(z)], sh, rh, zring(d)[1], t)
-    along_x(len(steps) - 1)
     bytes_of(v2.at[t, 0, c], rv1.at[1])
     push(v2.at[t, :, c], v2.at[t, :, c], sv3, rv3.at[0], sib, t)
 
@@ -326,28 +328,33 @@
     for n in range(1, nx - 1):
         part += respond_to(tiles[n], n)
     part += respond_to(tiles[nx - 1], nx - 1)
-    for k in range(nz):
-        cs[k] = part[:, 128 * k : 128 * k + 128].astype(COEF_LINK)
-    cr[z] = cs[z]
-    for d in zfar:
-        zz, gg = zring(d)
-        push(cs.at[zz], cr.at[z], sc, rc, gg, t)
-    bytes_of(cr.at[0 : nz - 1], rc)
-    done = cr[0].astype(F32)
-    for k in range(1, nz):
-        done = done + cr[k].astype(F32)
-    cw[s_me] = done.astype(B16)
-    top, bottom = done[0 : SL // 2], done[SL // 2 : SL]
-    cp[0] = jnp.where(half_lane, pltpu.roll(top, BLK, 1), bottom).astype(B16)
-    cp[1] = jnp.where(half_lane, top, pltpu.roll(bottom, BLK, 1)).astype(B16)
-
-    for dt in xfar:
-        tt = (t + dt) % nx
-        push(cp.at[0], cf.at[s_me], sd.at[1], rd.at[1], 2 * qup, tt)
-        push(cp.at[1], cf.at[s_me], sd.at[1], rd.at[1], 2 * qdown + 1, tt)
-        for dc in range(2):
-            if dc or dt:
-                push(cw.at[s_me], cw.at[s_me], sd.at[0], rd.at[0], 2 * q + (c + dc) % 2, tt)
+    rise = SL // HALVES
+    for h in range(HALVES):
+        for k in range(nz):
+            cs[h, k] = part[rise * h : rise * (h + 1), 128 * k : 128 * k + 128].astype(COEF_LINK)
+    for h in range(HALVES):
+        for d in zfar:
+            zz, gg = zring(d)
+            push(cs.at[h, zz], cr.at[h, z], sc, rc.at[h], gg, t)
+    quarter_lane = lax.broadcasted_iota(jnp.int32, (rise // 2, 128), 1) < BLK
+    for h in range(HALVES):
+        cr[h, z] = cs[h, z]
+        bytes_of(cr.at[h, 0 : nz - 1], rc.at[h])
+        done = cr[h, 0].astype(F32)
+        for k in range(1, nz):
+            done = done + cr[h, k].astype(F32)
+        cw[s_me, h] = done.astype(B16)
+        top, bottom = done[0 : rise // 2], done[rise // 2 : rise]
+        cp[0, h] = jnp.where(quarter_lane, pltpu.roll(top, BLK, 1), bottom).astype(B16)
+        cp[1, h] = jnp.where(quarter_lane, top, pltpu.roll(bottom, BLK, 1)).astype(B16)
+        for dt in xfar:
+            tt = (t + dt) % nx
+            push(cp.at[0, h], cf.at[s_me, h], sd.at[1], rd.at[1], 2 * qup, tt)
+            push(cp.at[1, h], cf.at[s_me, h], sd.at[1], rd.at[1], 2 * qdown + 1, tt)
+            for dc in range(2):
+                if dc or dt:
+                    mine = cw.at[s_me, h]
+                    push(mine, mine, sd.at[0], rd.at[0], 2 * q + (c + dc) % 2, tt)
     bytes_of(cw.at[0:7], rd.at[0])
     near = cw[...].reshape(8 * SL, 128)
     krow = lax.broadcasted_iota(jnp.int32, (BLK, 128), 0)
@@ -359,8 +366,9 @@
     bytes_of(cf, rd.at[1])
     pieces = []
     for k in range(8):
-        packed = cf[k]
-        pieces += [packed, pltpu.roll(packed.astype(F32), BLK, 1).astype(B16)]
+        for h in range(HALVES):
+            packed = cf[k, h]
+            pieces += [packed, pltpu.roll(packed.astype(F32), BLK, 1).astype(B16)]
     far = jnp.concatenate(pieces, axis=0)
     gmat[:, 128:256] = dot(occw[...], far).astype(B16)
 
@@ -389,7 +397,7 @@
     bytes_of(hz.at[:, 0 : 128 * (nz - 1)], sh)
     bytes_of(wr.at[:, 0 : ny - 1], sw)
     bytes_of(rz.at[:, 0 : (ny - 1) * share], sr)
-    bytes_of(cs.at[0 : nz - 1], sc)
+    bytes_of(cs.at[:, 0 : nz - 1], sc)
     bytes_of(cw.at[0:7], sd.at[0])
     bytes_of(cf, sd.at[1])
     give_c.wait()
@@ -429,13 +437,14 @@
         pltpu.VMEM((nx, 8, 16, 128), VIRT_LINK),
         pltpu.VMEM((nx, ny, 8 // ny, 16, 128), VIRT_LINK),
         pltpu.VMEM((nx, 8, 16, 128), B16),
-        pltpu.VMEM((nz, SL, 128), COEF_LINK),
-        pltpu.VMEM((nz, SL, 128), COEF_LINK),
-        pltpu.VMEM((8, SL, 128), B16),
-        pltpu.VMEM((8, SL // 2, 128), B16),
-        pltpu.VMEM((2, SL // 2, 128), B16),
+        pltpu.VMEM((HALVES, nz, SL // HALVES, 128), COEF_LINK),
+        pltpu.VMEM((HALVES, nz, SL // HALVES, 128), COEF_LINK),
+        pltpu.VMEM((8, HALVES, SL // HALVES, 128), B16),
+        pltpu.VMEM((8, HALVES, SL // HALVES // 2, 128), B16),
+        pltpu.VMEM((2, HALVES, SL // HALVES // 2, 128), B16),
         pltpu.VMEM((nx, BLK, WIN), B16),
-        dma((11,)),
+        pltpu.VMEM(virt.shape, B16),
+        dma((12,)),
         dma, dma((2,)),
         dma, dma((nz // 2 + 2,)),
         dma((2,)), dma((2, nz // 2 + 2)),
@@ -446,7 +455,7 @@
         dma, dma,
         dma, dma((4,)),
         dma, dma((4,)),
-        dma, dma,
+        dma, dma((HALVES,)),
         dma((2,)), dma((2,)),
         dma, dma((3,)),
     ]

time: 57.5 us -> 57.3 us (level)
  no operation moved by 1% of the time
where the time goes in v4:
time: 57.3 us; the launch traced here: 57.2 us
  Pallas kernels  56.5 us (99%)
  between operations  0.64 us (1%)
    pallas_call x1, Pallas kernels, per_device(): pl.pallas_call(functools.partial(kernel, topo), out_shape=(jax.ShapeDtype...  55.9 us

profile of v4, /device:TPU:1, one launch (start us, length us, event | category | flops | bytes accessed | tf_op | source)
XLA Modules:
  0.0 57.2 jit_solution(3790571307884695801)
XLA Ops:
  0.6 55.9 %dfpt_cycle.1 = (bf16[64,512]{1,0:T(8,128)(2,1)S(1)}, f32[24,256]{1,0:T(8,128)S(1)}) custom-call(bf16[24,256,128]{2,1,0:T(8,128)(2,1)} %basis_in.1, s32[2,24]{1,0:T(2,128)} %bitcast.4, s32[1,24]{1,0:T(1,128)} %bitcast.5, f32[24,256]{1,0:T(8,128)} %wpot_in.1, f32[24,256]{1,0:T(8,128)} %xc_in.1, bf16[64,512]{1,0:T(8,128)(2,1)} %occ.1, ...), custom_call_target="tpu_custom_call" | custom-call | tf_op jit(solution)/shard_map/dfpt_cycle/pallas_call | solution.py:462
  56.5 0.7 %hand_out.1 = (bf16[64,512]{1,0:T(8,128)(2,1)}, f32[24,256]{1,0:T(8,128)}) custom-call(bf16[64,512]{1,0:T(8,128)(2,1)S(1)} %get-tuple-element.4.coef, f32[24,256]{1,0:T(8,128)S(1)} %get-tuple-element.5.potential), custom_call_target="tpu_custom_call" | custom-call | tf_op jit(solution)/shard_map/hand_out/pallas_call | solution.py:480

commit v5 on v4

--- a/solution.py
+++ b/solution.py
@@ -37,8 +37,8 @@
     coef_out, dens_out,
     blocks, counts, basis, wpot, xc, eocc, evirt, coef, dens, gmat,
     occw, occt, bw, mat, ps, po, rb, ro, hz, v2, evb, eot, ws, wr, rz, cs, cr, cw, cf, cp, staged, virt,
-    sl, sa, ra, sv1, rv1, sv2, rv2, svf, rvf, sv3, rv3, se, re,
-    sb, rbs, sh, rh, sw, rw, sr, rr, sc, rc, sd, rd, ss, rs,
+    sl, sa, ra, sv1, rv1, rv2, rvf, sv3, rv3, se, re,
+    rbs, rh, rw, rr, rc, rd, ss, rs,
 ):
     nx, ny, nz = topo
     nq = ny * nz
@@ -132,7 +132,7 @@
     before = zring(nz - 1)
     chunk = virt.at[:, pl.ds(vstart(before[0]), WIN)]
     for k, to in enumerate((right, left)):
-        push(chunk, staged.at[t], sv2.at[k], rv2.at[k, 1], g, to)
+        push(chunk, staged.at[t], sv3, rv2.at[k, 1], g, to)
     for d in [nz // 2, 1] + znear[2:-1] + [nz - 1]:
         zz, gg = zring(d)
         group = group_of[nz - d]
@@ -173,7 +173,7 @@
         if k == 0:
             load_v.wait()
             for n, to in enumerate((right, left)):
-                push(v2.at[t, z, c], v2.at[t, z, c], sv2.at[n], rv2.at[n, 0], g, to)
+                push(v2.at[t, z, c], v2.at[t, z, c], sv3, rv2.at[n, 0], g, to)
 
     bytes_of(occw.at[pl.ds(pl.multiple_of(BLK * (1 - c), BLK), BLK)], ra.at[0])
     bytes_of(occw.at[far_rows], ra.at[1])
@@ -193,8 +193,8 @@
         bytes_of(v2.at[t, 0 : len(ds), c], rv1.at[n])
         for d in ds:
             mine = v2.at[t, (z + d) % nz, c]
-            push(mine, mine, sv2.at[0], rv2.at[0, n], g, right)
-            push(mine, mine, sv2.at[1], rv2.at[1, n], g, left)
+            push(mine, mine, sv3, rv2.at[0, n], g, right)
+            push(mine, mine, sv3, rv2.at[1, n], g, left)
 
     slot = 4 * c + t
     rb[slot] = ps[s_me]
@@ -203,17 +203,17 @@
         for dt in xfar:
             tt = (t + dt) % nx
             for cc in range(2):
-                push(po.at[tt * 2 + cc], ro.at[slot], sb.at[1], rbs.at[1], 2 * qother + cc, tt)
+                push(po.at[tt * 2 + cc], ro.at[slot], sa, rbs.at[1], 2 * qother + cc, tt)
             for dc in range(2):
                 if dc or dt:
                     cc = (c + dc) % 2
-                    push(ps.at[tt * 2 + cc], rb.at[slot], sb.at[0], rbs.at[0], 2 * q + cc, tt)
+                    push(ps.at[tt * 2 + cc], rb.at[slot], sv1, rbs.at[0], 2 * q + cc, tt)
 
     give_ham()
     for k, (frm, to) in enumerate(((left, right), (right, left))):
         bytes_of(staged.at[0], rv2.at[k, 1])
         if k == 1:
-            push(staged.at[frm], staged.at[frm], svf, rvf.at[0], g, to)
+            push(staged.at[frm], staged.at[frm], sv3, rvf.at[0], g, to)
         push(staged.at[frm], v2.at[frm, z, c], ss, rs.at[k], before[1], t)
     for n in range(2, len(steps)):
         along_x(n)
@@ -248,7 +248,7 @@
     zcols = lambda zz: pl.ds(pl.multiple_of(128 * zz, 128), 128)
     hz[:, zcols(z)] = ham.astype(B16)
     for d in zfar:
-        push(hz.at[:, zcols(z)], hz.at[:, zcols(z)], sh, rh, zring(d)[1], t)
+        push(hz.at[:, zcols(z)], hz.at[:, zcols(z)], sv1, rh, zring(d)[1], t)
     bytes_of(v2.at[t, 0, c], rv1.at[1])
     push(v2.at[t, :, c], v2.at[t, :, c], sv3, rv3.at[0], sib, t)
 
@@ -266,7 +266,7 @@
             for d in ds:
                 if (d in rightward) == (k == 0):
                     theirs = v2.at[frm, (z + d) % nz, c]
-                    push(theirs, theirs, svf, rvf.at[2 if n == len(steps) - 1 else 1], g, to)
+                    push(theirs, theirs, sv3, rvf.at[2 if n == len(steps) - 1 else 1], g, to)
             to_sibling(frm, 1 + k, ds)
     for k, frm in enumerate((left, right)):
         bytes_of(v2.at[frm, 0, c], rs.at[k])
@@ -284,7 +284,7 @@
         wr[n, y] = ws[n, pl.ds(y * share, share)]
         for d in yfar:
             yy, gg = yring(d)
-            push(ws.at[n, pl.ds(yy * share, share)], wr.at[n, y], sw, rw.at[n], gg, t)
+            push(ws.at[n, pl.ds(yy * share, share)], wr.at[n, y], sv1, rw.at[n], gg, t)
 
     def rotate(tt, n):
         bytes_of(wr.at[n, 0 : ny - 1], rw.at[n])
@@ -300,7 +300,7 @@
             rz[n, k] = jnp.where(repeat, 0.0, total / gap).astype(B16)
         mine = rz.at[n, pl.ds(y * share, share)]
         for d in yfar:
-            push(mine, mine, sr, rr.at[n], yring(d)[1], t)
+            push(mine, mine, sv1, rr.at[n], yring(d)[1], t)
 
     def respond_to(tt, n):
         bytes_of(rz.at[n, 0 : (ny - 1) * share], rr.at[n])
@@ -335,7 +335,7 @@
     for h in range(HALVES):
         for d in zfar:
             zz, gg = zring(d)
-            push(cs.at[h, zz], cr.at[h, z], sc, rc.at[h], gg, t)
+            push(cs.at[h, zz], cr.at[h, z], sv1, rc.at[h], gg, t)
     quarter_lane = lax.broadcasted_iota(jnp.int32, (rise // 2, 128), 1) < BLK
     for h in range(HALVES):
         cr[h, z] = cs[h, z]
@@ -349,12 +349,12 @@
         cp[1, h] = jnp.where(quarter_lane, top, pltpu.roll(bottom, BLK, 1)).astype(B16)
         for dt in xfar:
             tt = (t + dt) % nx
-            push(cp.at[0, h], cf.at[s_me, h], sd.at[1], rd.at[1], 2 * qup, tt)
-            push(cp.at[1, h], cf.at[s_me, h], sd.at[1], rd.at[1], 2 * qdown + 1, tt)
+            push(cp.at[0, h], cf.at[s_me, h], sa, rd.at[1], 2 * qup, tt)
+            push(cp.at[1, h], cf.at[s_me, h], sa, rd.at[1], 2 * qdown + 1, tt)
             for dc in range(2):
                 if dc or dt:
                     mine = cw.at[s_me, h]
-                    push(mine, mine, sd.at[0], rd.at[0], 2 * q + (c + dc) % 2, tt)
+                    push(mine, mine, sv1, rd.at[0], 2 * q + (c + dc) % 2, tt)
     bytes_of(cw.at[0:7], rd.at[0])
     near = cw[...].reshape(8 * SL, 128)
     krow = lax.broadcasted_iota(jnp.int32, (BLK, 128), 0)
@@ -384,22 +384,11 @@
 
     lax.fori_loop(0, groups, respond, 0)
     give_d = local(dens, dens_out, sl.at[1])
-    bytes_of(occw.at[0:128], sa)
-    bytes_of(v2.at[0, 0 : nz - 1, 0], sv1)
-    bytes_of(v2.at[0, :, 0], sv2.at[0])
-    bytes_of(v2.at[0, :, 0], sv2.at[1])
-    bytes_of(v2.at[0, :, 0], svf)
+    bytes_of(v2.at[0, :, 0], sa)
+    bytes_of(v2.at[:, 0 : nz - 1, 0], sv1)
+    bytes_of(v2.at[:, 0 : nz - 1], sv3)
     bytes_of(v2.at[0:3, 0, 0], ss)
-    bytes_of(v2.at[:, :, 0], sv3)
     bytes_of(evb.at[:, 0 : WIN * (nx - 1)], se)
-    bytes_of(rb.at[0:7], sb.at[0])
-    bytes_of(ro, sb.at[1])
-    bytes_of(hz.at[:, 0 : 128 * (nz - 1)], sh)
-    bytes_of(wr.at[:, 0 : ny - 1], sw)
-    bytes_of(rz.at[:, 0 : (ny - 1) * share], sr)
-    bytes_of(cs.at[:, 0 : nz - 1], sc)
-    bytes_of(cw.at[0:7], sd.at[0])
-    bytes_of(cf, sd.at[1])
     give_c.wait()
     give_d.wait()
 
@@ -447,16 +436,10 @@
         dma((12,)),
         dma, dma((2,)),
         dma, dma((nz // 2 + 2,)),
-        dma((2,)), dma((2, nz // 2 + 2)),
-        dma, dma((3,)),
+        dma((2, nz // 2 + 2)), dma((3,)),
         dma, dma((4,)),
         dma, dma,
-        dma((2,)), dma((2,)),
-        dma, dma,
-        dma, dma((4,)),
-        dma, dma((4,)),
-        dma, dma((HALVES,)),
-        dma((2,)), dma((2,)),
+        dma((2,)), dma, dma((4,)), dma((4,)), dma((HALVES,)), dma((2,)),
         dma, dma((3,)),
     ]
     coef, potential = pl.pallas_call(

time: 57.3 us -> 57.1 us (level)
  no operation moved by 1% of the time
where the time goes in v5:
time: 57.1 us; the launch traced here: 57 us
  Pallas kernels  56.3 us (99%)
  between operations  0.64 us (1%)
    pallas_call x1, Pallas kernels, per_device(): pl.pallas_call(functools.partial(kernel, topo), out_shape=(jax.ShapeDtype...  55.7 us

profile of v5, /device:TPU:1, one launch (start us, length us, event | category | flops | bytes accessed | tf_op | source)
XLA Modules:
  0.0 57.0 jit_solution(3954016358567214109)
XLA Ops:
  0.6 55.7 %dfpt_cycle.1 = (bf16[64,512]{1,0:T(8,128)(2,1)S(1)}, f32[24,256]{1,0:T(8,128)S(1)}) custom-call(bf16[24,256,128]{2,1,0:T(8,128)(2,1)} %basis_in.1, s32[2,24]{1,0:T(2,128)} %bitcast.4, s32[1,24]{1,0:T(1,128)} %bitcast.5, f32[24,256]{1,0:T(8,128)} %wpot_in.1, f32[24,256]{1,0:T(8,128)} %xc_in.1, bf16[64,512]{1,0:T(8,128)(2,1)} %occ.1, ...), custom_call_target="tpu_custom_call" | custom-call | tf_op jit(solution)/shard_map/dfpt_cycle/pallas_call | solution.py:445
  56.3 0.7 %hand_out.1 = (bf16[64,512]{1,0:T(8,128)(2,1)}, f32[24,256]{1,0:T(8,128)}) custom-call(bf16[64,512]{1,0:T(8,128)(2,1)S(1)} %get-tuple-element.4.coef, f32[24,256]{1,0:T(8,128)S(1)} %get-tuple-element.5.potential), custom_call_target="tpu_custom_call" | custom-call | tf_op jit(solution)/shard_map/hand_out/pallas_call | solution.py:463
